TPU v7x, 128 devices: a whole 4x4x4 slice. The times are simulated.
128 devices in a mesh: dp: 8 (over x, core), ctx: 4 (over y), tensor: 4 (over z).
Axes of the slice: x: 4, y: 4, z: 4, core: 2. Of those that a mesh axis runs over, the one named last changes fastest.
Arguments:
- hidden: bfloat16 [8, 16384, 2560], P('dp', 'ctx', 'tensor'), may hold values from -6 to 6
- depth: int32 [8, 16384], P('dp', 'ctx'), may hold values from 1 to 4, as said below
- qkv_weight: bfloat16 [2560, 3, 2560], P(None, None, 'tensor'), may hold values from -0.125 to 0.125
- out_weight: bfloat16 [2560, 2560], P('tensor'), may hold values from -0.125 to 0.125
Outputs:
- update: bfloat16 [8, 16384, 2560], P('dp', 'ctx', 'tensor')
Inputs may be any that keep to these rules, and one draw needn't show every extreme that they name: In every aligned block of 4096 positions of a document at most 1024 tokens have depth at least 3, and some block has exactly 1024; over all documents exactly 16384 tokens do.
All inputs are finite; a program needn't handle non-finite values.
Results may differ from a plain program's by a relative error of at most 0.012.
The roundings to bfloat16 on the way count: a program that leaves them out, or rounds other values in their place, can miss the bound.
Values may be sent and summed in bfloat16 or wider, within the bound.
No kernel may reach another device: no remote copies, remote signals or barrier semaphores. Data moves between devices by JAX's collectives and lax.ppermute only.
A program may use at most 256 MiB of HBM per device.

v0:
```python
import jax
import jax.numpy as jnp
from jax import lax
from jax.sharding import PartitionSpec as P

HD = 128
RECURSION = 3
ACT_DEV = 512
CAP = 1024


score_scale = 0.25
norm_epsilon = 1e-05
head_epsilon = 1e-06


def head_normed(values):
    row_count = values.shape[0]
    per_head = values.reshape(row_count, -1, HD)
    factor = lax.rsqrt(jnp.mean(per_head * per_head, axis=2, keepdims=True) + head_epsilon)
    return (per_head * factor).reshape(row_count, -1).astype(jnp.bfloat16)


def project_rows(token_rows, qkv_weight):
    full_rows = lax.all_gather(token_rows, "tensor", axis=1, tiled=True)
    widened = full_rows.astype(jnp.float32)
    factor = lax.rsqrt(jnp.mean(widened * widened, axis=1, keepdims=True) + norm_epsilon)
    normed = (widened * factor).astype(jnp.bfloat16)
    head_width = qkv_weight.shape[2]
    projection = jnp.dot(
        normed,
        qkv_weight.reshape(qkv_weight.shape[0], 3 * head_width),
        preferred_element_type=jnp.float32,
    )
    queries = head_normed(projection[:, :head_width])
    keys_normed = head_normed(projection[:, head_width : 2 * head_width])
    values_out = projection[:, 2 * head_width :].astype(jnp.bfloat16)
    return jnp.concatenate([queries, keys_normed, values_out], axis=1)


def output_rows(context, out_weight):
    partial_value = jnp.dot(context, out_weight, preferred_element_type=jnp.float32)
    return lax.psum_scatter(
        partial_value.astype(jnp.bfloat16), "tensor", scatter_dimension=1, tiled=True
    )


def move_tiles(payload):
    return lax.all_to_all(payload, ("dp", "ctx"), split_axis=0, concat_axis=0, tiled=True)


def per_device(hidden, depth, qkv_weight, out_weight):
    tokens = hidden[0]
    local_len = tokens.shape[0]
    feature_width = tokens.shape[1]
    capacity = CAP
    head_width = out_weight.shape[0]
    heads_here = head_width // HD
    ctx_count = lax.axis_size("ctx")
    spread_size = lax.axis_size("dp") * ctx_count
    ctx_rank = lax.axis_index("ctx")
    my_index = lax.axis_index("dp") * ctx_count + ctx_rank
    active = (depth[0] >= RECURSION).astype(jnp.int32)
    active_count = jnp.sum(active)
    active_rank = jnp.cumsum(active) - 1
    slot_token = (
        jnp.zeros((capacity,), jnp.int32)
        .at[jnp.where(active > 0, active_rank, capacity)]
        .set(jnp.arange(local_len, dtype=jnp.int32), mode="drop")
    )
    filled = jnp.arange(capacity, dtype=jnp.int32) < active_count
    token_rows = jnp.where(filled[:, None], tokens[slot_token], jnp.zeros((), tokens.dtype))
    counts = lax.all_gather(active_count[None], ("dp", "ctx"), axis=0, tiled=True)
    doc_counts = lax.dynamic_slice_in_dim(counts, lax.axis_index("dp") * ctx_count, ctx_count)
    slot_size = capacity // spread_size
    offsets = jnp.cumsum(counts) - counts
    first_rank = offsets[my_index]
    global_rank = first_rank + jnp.arange(capacity, dtype=jnp.int32)
    target = global_rank % spread_size
    position = (
        global_rank // spread_size
        - first_rank // spread_size
        - (target < first_rank % spread_size).astype(jnp.int32)
    )
    send_at = jnp.where(filled, target * slot_size + position, capacity)
    fetch_at = jnp.minimum(send_at, capacity - 1)
    lower_bound = (offsets - my_index + spread_size - 1) // spread_size
    upper_bound = (offsets + counts - my_index + spread_size - 1) // spread_size
    arrived = (
        jnp.arange(slot_size, dtype=jnp.int32)[None, :] < (upper_bound - lower_bound)[:, None]
    ).reshape(-1)
    arrived_rank = jnp.cumsum(arrived.astype(jnp.int32)) - 1
    chosen = (
        jnp.zeros((ACT_DEV,), jnp.int32)
        .at[jnp.where(arrived, arrived_rank, ACT_DEV)]
        .set(jnp.arange(capacity, dtype=jnp.int32), mode="drop")
    )
    packed = (
        jnp.zeros((capacity,) + token_rows.shape[1:], token_rows.dtype)
        .at[send_at]
        .set(token_rows, mode="drop")
    )
    values = project_rows(move_tiles(packed)[chosen], qkv_weight)
    bring_packed = jnp.zeros((capacity,) + values.shape[1:], values.dtype).at[chosen].set(values)
    projected = move_tiles(bring_packed)[fetch_at]
    queries = projected[:, :head_width]
    key_values = projected[:, head_width:]
    query_heads = queries.reshape(capacity, heads_here, HD)
    key_piece = lax.all_gather(key_values, "ctx", axis=0, tiled=True)
    piece_rows = key_piece.shape[0]
    row_index = jnp.arange(piece_rows, dtype=jnp.int32)
    source_shard = row_index // capacity
    source_slot = row_index - source_shard * capacity
    clipped = jnp.clip(source_shard, 0, ctx_count - 1)
    key_filled = (source_shard >= 0) & (source_slot < doc_counts[clipped])
    same_block = (source_shard == ctx_rank)[None, :] & (
        slot_token[source_slot][None, :] <= slot_token[:, None]
    )
    earlier = (source_shard < ctx_rank)[None, :] | same_block
    allowed = earlier & key_filled[None, :] & filled[:, None]
    key_heads = key_piece[:, :head_width].reshape(piece_rows, heads_here, HD)
    value_heads = key_piece[:, head_width:].reshape(piece_rows, heads_here, HD)
    scores = (
        jnp.einsum("qhd,khd->hqk", query_heads, key_heads, preferred_element_type=jnp.float32)
        * score_scale
    )
    weights = jnp.where(allowed[None], jnp.exp(scores), 0.0)
    numerator = jnp.einsum(
        "hqk,khd->qhd",
        weights.astype(jnp.bfloat16),
        value_heads,
        preferred_element_type=jnp.float32,
    )
    denominator = jnp.sum(weights, axis=2)
    numerator, denominator = (numerator, denominator)
    guarded = denominator + (1.0 - filled.astype(jnp.float32))[None, :]
    context = (
        (numerator / jnp.transpose(guarded)[:, :, None])
        .reshape(capacity, head_width)
        .astype(jnp.bfloat16)
    )
    result_rows = output_rows(context, out_weight)
    update = (
        jnp.zeros((local_len, feature_width), jnp.bfloat16)
        .at[jnp.where(filled, slot_token, local_len)]
        .set(result_rows, mode="drop")
    )
    return update[None]


def solution(mesh):
    placed = (P("dp", "ctx", "tensor"), P("dp", "ctx"), P(None, None, "tensor"), P("tensor", None))
    return jax.shard_map(
        per_device, mesh=mesh, in_specs=placed, out_specs=P("dp", "ctx", "tensor"), check_vma=False
    )
```

profile of v0, /device:TPU:1, one launch (start us, length us, event | category | flops | bytes accessed | tf_op | source)
XLA Modules:
  0.0 554.7 jit_solution(16296913542401398679)
XLA Ops:
  11.6 16.9 %all-reduce = s32[32]{0:T(128)S(1)} all-reduce(s32[32]{0:T(128)S(1)} %dynamic-update-slice), channel_id=1, replica_groups=mesh['dp'=8,'ctx'=4,'tensor'=4] {'dp','ctx'}, use_global_device_ids=true, to_apply=%add | all-reduce | flops 32 | bytes 256
  33.9 15.5 %scatter_custom_fusion = s32[1024]{0:T(1024)S(1)} fusion(s32[4096]{0:T(1024)S(1)} %bitcast.67, s32[4096]{0:T(1024)S(1)} %iota.52, s32[]{:T(128)} %constant.133.clone.1), kind=kCustom, calls=%fused_computation.99 | custom fusion | bytes 4100 | tf_op jit(solution)/shard_map/scatter | solution.py:69
  52.0 19.1 %scatter_custom_fusion.2 = bf16[1024,640]{1,0:T(8,128)(2,1)} fusion(s32[1024]{0:T(1024)S(1)} %bitcast.71, pred[1024]{0:T(1024)(128)(4,1)S(1)} %iota_compare_fusion.1, bf16[]{:T(256)} %constant.131.clone.1, bf16[4096,640]{1,0:T(8,128)(2,1)} %bitcast.59, s32[1024]{0:T(1024)S(1)} %get-tuple-element.13), kind=kCustom, calls=%fused_computation.37 | custom fusion | flops 655360 | bytes 6559744 | tf_op jit(solution)/shard_map/scatter | solution.py:101
  71.1 30.9 %all-to-all-start = ((bf16[32,32,640]{2,1,0:T(8,128)(2,1)}), bf16[32,32,640]{2,1,0:T(8,128)(2,1)}, u32[]{:S(2)}, u32[]{:S(2)}) async-start(bf16[32,32,640]{2,1,0:T(8,128)(2,1)} %bitcast.60), calls=%async_computation | async-start | bytes 2621440 | tf_op jit(solution)/shard_map/all_to_all | solution.py:49
  103.2 4.5 scatter_custom_fusion.1
  107.7 13.3 %all-to-all-done = bf16[32,32,640]{2,1,0:T(8,128)(2,1)} async-done(((bf16[32,32,640]{2,1,0:T(8,128)(2,1)}), bf16[32,32,640]{2,1,0:T(8,128)(2,1)}, u32[]{:S(2)}, u32[]{:S(2)}) %all-to-all-start) | async-done | bytes 1310752 | tf_op jit(solution)/shard_map/all_to_all | solution.py:49
  121.0 4.3 gather_fusion
  125.3 13.9 %copy.19 = bf16[2560,3,640]{0,2,1:T(8,128)(2,1)} copy(bf16[2560,3,640]{2,0,1:T(8,128)(2,1)} %param.6) | data formatting | bytes 19660800 | tf_op args[2]
  139.1 21.2 %all-gather.6.cloned.1.call-done = bf16[512,2560]{1,0:T(8,128)(2,1)} async-done(((bf16[512,640]{1,0:T(8,128)(2,1)}), bf16[512,2560]{1,0:T(8,128)(2,1)}) %all-gather.6.cloned.1.call-update) | async-done | bytes 2621456 | tf_op jit(solution)/shard_map/all_gather | solution.py:25
  162.7 9.3 %fusion.7 = f32[512,1920]{1,0:T(8,128)S(1)} fusion(bf16[2560,1920]{0,1:T(8,128)(2,1)} %bitcast.52, bf16[512,2560]{1,0:T(8,128)(2,1)} %all-gather.6.cloned.1.call-done, f32[512]{0:T(512)S(1)} %add_rsqrt_fusion.2), kind=kOutput, calls=%fused_computation.20 | convolution fusion | flops 5037096960 | bytes 16386048 | tf_op jit(solution)/shard_map/dot_general | solution.py:30
  175.8 2.8 copy.20
  181.3 2.8 copy.21
  184.0 2.8 copy.22
  189.6 2.8 copy.23
  192.4 3.8 multiply_convert_fusion.1
  196.2 7.0 %scatter_custom_fusion.3 = bf16[1024,1920]{1,0:T(8,128)(2,1)} fusion(s32[512]{0:T(512)S(1)} %compare_select_fusion.15, bf16[512,640]{1,0:T(8,128)(2,1)} %slice.81, bf16[]{:T(256)} %constant.171, bf16[512,640]{1,0:T(8,128)(2,1)} %get-tuple-element.10, bf16[512,640]{1,0:T(8,128)(2,1)} %get-tuple-element.9, bf16[]{:T(256)} %constant.131.clone.1), kind=kCustom, calls=%fused_computation.26 | custom fusion | flops 5898240 | bytes 5898244 | tf_op jit(solution)/shard_map/scatter | solution.py:104
  203.2 7.8 %all-to-all-start.1 = ((bf16[32,32,1920]{2,1,0:T(8,128)(2,1)}), bf16[32,32,1920]{2,1,0:T(8,128)(2,1)}, u32[]{:S(2)}, u32[]{:S(2)}) async-start(bf16[32,32,1920]{2,1,0:T(8,128)(2,1)} %bitcast.51), calls=%async_computation.1 | async-start | bytes 7864320 | tf_op jit(solution)/shard_map/all_to_all | solution.py:49
  211.0 47.3 %all-to-all-done.1 = bf16[32,32,1920]{2,1,0:T(8,128)(2,1)} async-done(((bf16[32,32,1920]{2,1,0:T(8,128)(2,1)}), bf16[32,32,1920]{2,1,0:T(8,128)(2,1)}, u32[]{:S(2)}, u32[]{:S(2)}) %all-to-all-start.1) | async-done | bytes 3932192 | tf_op jit(solution)/shard_map/all_to_all | solution.py:49
  258.3 11.1 %gather_fusion.1 = bf16[1024,1920]{1,0:T(8,128)(2,1)} fusion(bf16[1024,1920]{1,0:T(8,128)(2,1)} %bitcast.20, s32[1024]{0:T(1024)S(1)} %broadcast_clamp_fusion.1), kind=kCustom, calls=%fused_computation.2 | custom fusion | bytes 7868416 | tf_op jit(solution)/shard_map/gather | solution.py:105
  269.4 3.4 slice.66
  273.0 16.7 %gather_fusion.2 = s32[4096]{0:T(1024)S(1)} fusion(s32[1024]{0:T(1024)S(1)} %scatter_custom_fusion, s32[4096]{0:T(1024)S(1)} %broadcast_clamp_fusion), kind=kCustom, calls=%fused_computation.3 | custom fusion | bytes 49152 | tf_op jit(solution)/shard_map/gather | solution.py:117
  293.5 6.2 %and_and_fusion = pred[1024,4096]{1,0:T(8,128)(4,1)} fusion(s32[4096]{0:T(1024)S(1)} %gather_fusion.2, s32[1024]{0:T(1024)S(1)} %scatter_custom_fusion, pred[1024]{0:T(1024)(128)(4,1)S(1)} %iota_compare_fusion.1, pred[4096]{0:T(1024)(128)(4,1)S(1)} %fusion.32, pred[4096]{0:T(1024)(128)(4,1)S(1)} %get-tuple-element.23, pred[4096]{0:T(1024)(128)(4,1)S(1)} %get-tuple-element.24), kind=kLoop, calls=%fused_computation.14 | loop fusion | flops 20971520 | bytes 4228096 | tf_op jit(solution)/shard_map/and | solution.py:120
  304.7 69.3 %all-gather.4.cloned.1.call-done = bf16[4096,1280]{1,0:T(8,128)(2,1)} async-done(((bf16[1024,1280]{1,0:T(8,128)(2,1)}), bf16[4096,1280]{1,0:T(8,128)(2,1)}) %all-gather.4.cloned.1.call-update) | async-done | bytes 10485776 | tf_op jit(solution)/shard_map/all_gather | solution.py:109
  373.9 9.0 %fusion.46 = (bf16[4096,640]{1,0:T(8,128)(2,1)}, bf16[4096,640]{1,0:T(8,128)(2,1)}) fusion(bf16[4096,1280]{1,0:T(8,128)(2,1)} %all-gather.4.cloned.1.call-done), kind=kLoop, calls=%fused_computation.116 | loop fusion | bytes 20971520 | tf_op jit(solution)/shard_map/slice | solution.py:121
  383.0 7.9 %copy.24 = bf16[4096,640]{0,1:T(8,128)(2,1)} copy(bf16[4096,640]{1,0:T(8,128)(2,1)} %get-tuple-element.8) | data formatting | bytes 10485760 | tf_op jit(solution)/shard_map/slice | solution.py:122
  390.9 8.0 %copy.26 = bf16[4096,640]{0,1:T(8,128)(2,1)} copy(bf16[4096,640]{1,0:T(8,128)(2,1)} %get-tuple-element.7) | data formatting | bytes 10485760 | tf_op jit(solution)/shard_map/slice | solution.py:121
  398.9 36.3 %fusion = (f32[5,1024]{1,0:T(8,128)S(1)}, f32[5,1024,4096]{2,1,0:T(8,128)}) fusion(pred[1024,4096]{1,0:T(8,128)(4,1)} %and_and_fusion, bf16[1024,5,128]{0,2,1:T(8,128)(2,1)} %bitcast.61, bf16[4096,5,128]{0,2,1:T(8,128)(2,1)} %bitcast.54), kind=kOutput, calls=%fused_computation.10 | convolution fusion | flops 5431618560 | bytes 94654464 | tf_op jit(solution)/shard_map/qhd,khd->hqk/dot_general | solution.py:124
  435.2 30.0 %fusion.9 = bf16[1024,5,128]{0,2,1:T(8,128)(2,1)S(1)} fusion(bf16[4096,5,128]{0,2,1:T(8,128)(2,1)} %bitcast.53, f32[5,1024,4096]{2,1,0:T(8,128)} %get-tuple-element.20, pred[1024,4096]{1,0:T(8,128)(4,1)} %and_and_fusion, f32[1024,5]{0,1:T(8,128)S(1)} %add_bitcast_fusion), kind=kOutput, calls=%fused_computation.22 | convolution fusion | flops 5432934400 | bytes 94654464 | tf_op jit(solution)/shard_map/hqk,khd->qhd/dot_general | solution.py:128
  465.2 6.3 %convolution_convert_fusion = bf16[1024,2560]{1,0:T(8,128)(2,1)} fusion(bf16[1024,640]{0,1:T(8,128)(2,1)S(1)} %bitcast.73, bf16[640,2560]{1,0:T(8,128)(2,1)S(1)} %copy-done), kind=kOutput, calls=%fused_computation.17 | convolution fusion | flops 3358064640 | bytes 9830400 | tf_op jit(solution)/shard_map/dot_general | solution.py:42
  471.5 8.0 %copy.31 = bf16[1024,2560]{0,1:T(8,128)(2,1)} copy(bf16[1024,2560]{1,0:T(8,128)(2,1)} %convolution_convert_fusion) | data formatting | bytes 10485760
  479.5 56.8 %reduce-scatter.4.cloned.1.call-done = bf16[640,1024]{1,0:T(8,128)(2,1)} async-done(((bf16[2560,1024]{1,0:T(8,128)(2,1)}), bf16[640,1024]{1,0:T(8,128)(2,1)}) %reduce-scatter.4.cloned.1.call-update) | async-done | bytes 1310736
  538.8 9.0 %scatter_custom_fusion.4 = bf16[4096,640]{1,0:T(8,128)(2,1)} fusion(s32[1024]{0:T(1024)} %get-tuple-element.14, bf16[1024,640]{1,0:T(8,128)(2,1)} %copy.32, bf16[]{:T(256)} %constant.131.clone.1), kind=kCustom, calls=%fused_computation.24 | custom fusion | bytes 5243392 | tf_op jit(solution)/shard_map/scatter | solution.py:146
  (70 shorter events, 34.4 us)
Async XLA Ops:
  6.5 458.7 %copy-start = (bf16[640,2560]{1,0:T(8,128)(2,1)S(1)}, bf16[640,2560]{1,0:T(8,128)(2,1)}, u32[]{:S(2)}) copy-start(bf16[640,2560]{1,0:T(8,128)(2,1)} %param.7) | copy-start | bytes 9830404
  71.1 49.9 %all-to-all-start = ((bf16[32,32,640]{2,1,0:T(8,128)(2,1)}), bf16[32,32,640]{2,1,0:T(8,128)(2,1)}, u32[]{:S(2)}, u32[]{:S(2)}) async-start(bf16[32,32,640]{2,1,0:T(8,128)(2,1)} %bitcast.60), calls=%async_computation | async-start | bytes 2621440 | tf_op jit(solution)/shard_map/all_to_all | solution.py:49
  102.0 58.3 %all-gather.6.cloned.1.call-start = ((), (), s32[]{:S(2)}) async-start(), calls=%async_computation.4 | async-start | bytes 3276800 | tf_op jit(solution)/shard_map/all_gather | solution.py:25
  171.9 2.1 copy-start.1
  203.2 55.2 %all-to-all-start.1 = ((bf16[32,32,1920]{2,1,0:T(8,128)(2,1)}), bf16[32,32,1920]{2,1,0:T(8,128)(2,1)}, u32[]{:S(2)}, u32[]{:S(2)}) async-start(bf16[32,32,1920]{2,1,0:T(8,128)(2,1)} %bitcast.51), calls=%async_computation.1 | async-start | bytes 7864320 | tf_op jit(solution)/shard_map/all_to_all | solution.py:49
  211.0 163.0 %all-gather.4.cloned.1.call-start = ((), (), s32[]{:S(2)}) async-start(), calls=%async_computation.3 | async-start | bytes 13107200 | tf_op jit(solution)/shard_map/all_gather | solution.py:109
  272.9 263.4 %reduce-scatter.4.cloned.1.call-start = ((), (), s32[]{:S(2)}) async-start(), calls=%async_computation.5 | async-start | bytes 6553600
Sparse Core Ops, SparseCore 0:
  125.4 34.8 all-gather.5
  273.0 100.8 all-gather.3
  479.6 56.6 reduce-scatter.3
where the time goes:
time: 563 us; the launch traced here: 555 us
  waiting for transfers between devices  208 us (37%)
  local copies, waits for them, and re-layouts  139 us (25%)
  matrix products  81.8 us (15%)
  other arithmetic  53.5 us (10%)
  starting transfers between devices  38.8 us (7%)
  blocking collectives  16.9 us (3%)
  between operations  16.4 us (3%)
    all_gather x1, waiting for transfers between devices, per_device(): key_piece = lax.all_gather(key_values, 'ctx', axis=0, tiled=True)  69.3 us
    all_to_all x2, waiting for transfers between devices, move_tiles(): lax.all_to_all(payload, ('dp', 'ctx'), split_axis=0, concat_axis=0, tiled...  60.6 us
    unnamed x4, waiting for transfers between devices  56.9 us
    all_to_all x2, starting transfers between devices, move_tiles(): lax.all_to_all(payload, ('dp', 'ctx'), split_axis=0, concat_axis=0, tiled...  38.7 us
    dot_general x1, matrix products, per_device(): jnp.einsum('qhd,khd->hqk', query_heads, key_heads, preferred_element_type...  36.3 us
    dot_general x1, matrix products, per_device(): jnp.einsum('hqk,khd->qhd', weights.astype(jnp.bfloat16), value_heads, pre...  30 us
    unnamed x10, local copies, waits for them, and re-layouts  28 us
    all_gather x1, waiting for transfers between devices, project_rows(): full_rows = lax.all_gather(token_rows, 'tensor', axis=1, tiled=True)  21.2 us
  transfers between devices with their start and end apart: 5, of which 5 were waited for; matrix products, arithmetic and copies ran while one was open for 9% of the time, Pallas kernels for 0%

commit v1 on v0

v1 whole, which is shorter than its diff:
```python
import math

import jax
import jax.numpy as jnp
from jax import lax
from jax.experimental import pallas as pl
from jax.experimental.pallas import tpu as pltpu
from jax.sharding import PartitionSpec as P

HD = 128
RECURSION = 3
CAP = 1024
HALF = CAP // 2
SUB = CAP // 4
TOK_BLOCK = 256
WINDOW = 384
ROOM = CAP + WINDOW

score_scale = 0.25
norm_epsilon = 1e-05
head_epsilon = 1e-06
EXP2_SCALE = score_scale / math.log(2.0)
VMEM_LIMIT = 56 * 1024 * 1024

bf16 = jnp.bfloat16
f32 = jnp.float32


def params(**more):
    return pltpu.CompilerParams(vmem_limit_bytes=VMEM_LIMIT, **more)


def slot_onehot(depth_row, shift):
    active = depth_row >= RECURSION
    flags = jnp.broadcast_to(jnp.where(active, 1.0, 0.0), (8, TOK_BLOCK)).astype(bf16)
    before = lax.broadcasted_iota(jnp.int32, (TOK_BLOCK, TOK_BLOCK), 0)
    after = lax.broadcasted_iota(jnp.int32, (TOK_BLOCK, TOK_BLOCK), 1)
    earlier = jnp.where(before < after, 1.0, 0.0).astype(bf16)
    rank = jnp.dot(flags, earlier, preferred_element_type=f32)[0:1].astype(jnp.int32)
    slot = jnp.where(active, rank + shift, -1)
    rows = lax.broadcasted_iota(jnp.int32, (WINDOW, TOK_BLOCK), 0)
    return jnp.where(rows == slot, 1.0, 0.0).astype(bf16)


def window_start(offset):
    return pl.multiple_of((offset >> 7) << 7, 128)


def compact_kernel(offs_ref, depth_ref, tok_ref, o0, o1, o2, o3, buf):
    step = pl.program_id(0)

    @pl.when(step == 0)
    def _():
        buf[...] = jnp.zeros_like(buf)

    for sub in range(2):
        offset = offs_ref[step * 2 + sub]
        start = window_start(offset)
        onehot = slot_onehot(depth_ref[sub], offset - start)
        picked = jnp.dot(
            onehot,
            tok_ref[sub * TOK_BLOCK : (sub + 1) * TOK_BLOCK, :],
            preferred_element_type=f32,
        ).astype(bf16)
        buf[pl.ds(start, WINDOW), :] = buf[pl.ds(start, WINDOW), :] + picked

    @pl.when(step == pl.num_programs(0) - 1)
    def _():
        for i, o in enumerate((o0, o1, o2, o3)):
            o[...] = buf[i * SUB : (i + 1) * SUB, :]


def compact_rows(tokens, depth_blocks, offsets):
    length, width = tokens.shape
    steps = length // (2 * TOK_BLOCK)
    sub = jax.ShapeDtypeStruct((SUB, width), bf16)
    return pl.pallas_call(
        compact_kernel,
        out_shape=(sub,) * 4,
        grid_spec=pltpu.PrefetchScalarGridSpec(
            num_scalar_prefetch=1,
            grid=(steps,),
            in_specs=[
                pl.BlockSpec((2, 1, TOK_BLOCK), lambda i, o: (i, 0, 0)),
                pl.BlockSpec((2 * TOK_BLOCK, width), lambda i, o: (i, 0)),
            ],
            out_specs=(pl.BlockSpec((SUB, width), lambda i, o: (0, 0)),) * 4,
            scratch_shapes=[pltpu.VMEM((ROOM, width), bf16)],
        ),
        compiler_params=params(),
        name="compact",
    )(offsets, depth_blocks, tokens)


def project_kernel(
    place, x0, x1, a0, a1, b0, b1, c0, d1, w_ref, o0, o1, o2, o3, q4, kv4, xs, acc
):
    part = pl.program_id(0)
    t = place[0]
    ctx = place[1]
    width = x0.shape[1]

    @pl.when(part == 0)
    def _():
        for sub, pieces in enumerate(((x0, a0, b0, c0), (x1, a1, b1, d1))):
            squares = jnp.zeros((SUB, 1), f32)
            for piece in pieces:
                wide = piece[...].astype(f32)
                squares = squares + jnp.sum(wide * wide, axis=1, keepdims=True)
            factor = lax.rsqrt(squares * (1.0 / (4 * width)) + norm_epsilon)
            for shift, piece in zip((0, 3, 1, 2), pieces):
                lane = pl.multiple_of(((t + shift) & 3) * width, 128)
                normed = (piece[...].astype(f32) * factor).astype(bf16)
                xs[sub * SUB : (sub + 1) * SUB, pl.ds(lane, width)] = normed

    acc[...] = jnp.dot(xs[...], w_ref[...], preferred_element_type=f32)
    for slot, out in enumerate((o0, o1, o2, o3, None)):
        if out is None:
            y = acc[:, 4 * HD : 5 * HD]
        else:
            y = acc[:, pl.ds(pl.multiple_of(((ctx + slot) & 3) * HD, HD), HD)]
        scale = lax.rsqrt(jnp.mean(y * y, axis=1, keepdims=True) + head_epsilon)
        z = (y * jnp.where(part == 2, 1.0, scale)).astype(bf16)
        if out is None:

            @pl.when(part == 0)
            def _():
                q4[...] = z

            @pl.when(part > 0)
            def _():
                kv4[0] = z

        else:
            out[0] = z


def project(place, own, left, right, far, weight):
    width = own[0].shape[1]
    model = 4 * width
    sub = pl.BlockSpec((SUB, width), lambda j, p: (0, 0))
    stacked = jax.ShapeDtypeStruct((3, HALF, HD), bf16)
    stacked_spec = pl.BlockSpec((1, HALF, HD), lambda j, p: (j, 0, 0))
    return pl.pallas_call(
        project_kernel,
        out_shape=(stacked,) * 4
        + (
            jax.ShapeDtypeStruct((HALF, HD), bf16),
            jax.ShapeDtypeStruct((2, HALF, HD), bf16),
        ),
        grid_spec=pltpu.PrefetchScalarGridSpec(
            num_scalar_prefetch=1,
            grid=(3,),
            in_specs=[sub] * 8 + [pl.BlockSpec((model, 5 * HD), lambda j, p: (0, j))],
            out_specs=(stacked_spec,) * 4
            + (
                pl.BlockSpec((HALF, HD), lambda j, p: (0, 0)),
                pl.BlockSpec((1, HALF, HD), lambda j, p: (jnp.maximum(j - 1, 0), 0, 0)),
            ),
            scratch_shapes=[
                pltpu.VMEM((HALF, model), bf16),
                pltpu.VMEM((HALF, 5 * HD), f32),
            ],
        ),
        compiler_params=params(),
        name="project",
    )(place, *own, *left, *right, *far, weight)


def attend_chunk(chunk, query, count_of, ks, vs, acc):
    def add_tile(key_chunk, masked):
        scores = lax.dot_general(
            query, ks[key_chunk], (((1,), (1,)), ((), ())), preferred_element_type=f32
        )
        weights = jnp.exp2(scores * EXP2_SCALE)
        if masked:
            row = lax.broadcasted_iota(jnp.int32, (HALF, HALF), 0)
            col = lax.broadcasted_iota(jnp.int32, (HALF, HALF), 1)
            weights = jnp.where(col <= row, weights, 0.0)
        acc[...] += jnp.dot(weights.astype(bf16), vs[key_chunk], preferred_element_type=f32)

    acc[...] = jnp.zeros_like(acc)

    def body(key_chunk, carry):
        @pl.when(count_of(key_chunk >> 1) > (key_chunk & 1) * HALF)
        def _():
            add_tile(key_chunk, False)

        return carry

    lax.fori_loop(0, chunk, body, 0)
    add_tile(chunk, True)
    total = acc[:, HD:]
    return (acc[:, :HD] / jnp.where(total == 0.0, 1.0, total)).astype(bf16)


def value_rows(value, half, count):
    rows = lax.broadcasted_iota(jnp.int32, (HALF, HD), 0) + half * HALF
    return value, jnp.where(rows < count, 1.0, 0.0).astype(bf16)


def attend_main_kernel(place, *refs):
    inputs, outs, (qs, ks, vs, cs, acc) = refs[:8], refs[8:16], refs[16:]
    ctx = place[0]

    def count_of(block):
        return place[1 + ((ctx - block) & 3)]

    for s in range(4):
        block = (ctx - s) & 3
        for half in range(2):
            chunk = block * 2 + half
            source = inputs[2 * s + half]
            qs[chunk] = source[0]
            ks[chunk] = source[1]
            value, flag = value_rows(source[2], half, place[1 + s])
            vs[chunk, :, :HD] = value
            vs[chunk, :, HD:] = flag

    def body(chunk, carry):
        filled = count_of(chunk >> 1) > (chunk & 1) * HALF

        @pl.when(filled)
        def _():
            cs[chunk] = attend_chunk(chunk, qs[chunk], count_of, ks, vs, acc)

        @pl.when(jnp.logical_not(filled))
        def _():
            cs[chunk] = jnp.zeros((HALF, HD), bf16)

        return carry

    lax.fori_loop(0, 8, body, 0)
    for s in range(4):
        for half in range(2):
            outs[2 * s + half][...] = cs[((ctx - s) & 3) * 2 + half]


def vmem_specs(count):
    return [pl.BlockSpec(memory_space=pltpu.VMEM)] * count


def attend_main(place, inputs):
    return pl.pallas_call(
        attend_main_kernel,
        out_shape=(jax.ShapeDtypeStruct((HALF, HD), bf16),) * 8,
        in_specs=[pl.BlockSpec(memory_space=pltpu.SMEM)] + vmem_specs(8),
        out_specs=tuple(vmem_specs(8)),
        scratch_shapes=[
            pltpu.VMEM((8, HALF, HD), bf16),
            pltpu.VMEM((8, HALF, HD), bf16),
            pltpu.VMEM((8, HALF, 2 * HD), bf16),
            pltpu.VMEM((8, HALF, HD), bf16),
            pltpu.VMEM((HALF, 2 * HD), f32),
        ],
        compiler_params=params(),
        name="attend_main",
    )(place, *inputs)


def attend_last_kernel(place, q0, q1, kv0, kv1, o0, o1, ks, vs, acc):
    ctx = place[0]

    def count_of(block):
        return place[1 + ((ctx - block) & 3)]

    for block in range(4):

        @pl.when(block <= ctx)
        def _():
            for half, source in enumerate((kv0, kv1)):
                chunk = block * 2 + half
                ks[chunk] = source[block, 0]
                value, flag = value_rows(source[block, 1], half, count_of(block))
                vs[chunk, :, :HD] = value
                vs[chunk, :, HD:] = flag

    for half, (query, out) in enumerate(((q0, o0), (q1, o1))):
        filled = place[1] > half * HALF

        @pl.when(filled)
        def _():
            out[...] = attend_chunk(ctx * 2 + half, query[...], count_of, ks, vs, acc)

        @pl.when(jnp.logical_not(filled))
        def _():
            out[...] = jnp.zeros((HALF, HD), bf16)


def attend_last(place, queries, gathered):
    return pl.pallas_call(
        attend_last_kernel,
        out_shape=(jax.ShapeDtypeStruct((HALF, HD), bf16),) * 2,
        in_specs=[pl.BlockSpec(memory_space=pltpu.SMEM)] + vmem_specs(4),
        out_specs=tuple(vmem_specs(2)),
        scratch_shapes=[
            pltpu.VMEM((8, HALF, HD), bf16),
            pltpu.VMEM((8, HALF, 2 * HD), bf16),
            pltpu.VMEM((HALF, 2 * HD), f32),
        ],
        compiler_params=params(),
        name="attend_last",
    )(place, *queries, *gathered)


def output_kernel(offs_ref, depth_ref, *refs):
    groups, weights, (out, cbuf, rows) = refs[:15], refs[15:19], refs[19:]
    step = pl.program_id(0)

    @pl.when(step == 0)
    def _():
        rows[CAP:, :] = jnp.zeros((WINDOW, rows.shape[1]), bf16)
        for half in range(2):
            total = None
            for source in range(4):
                first = groups[:5]
                rest = groups[5 + 5 * half : 10 + 5 * half]
                if source < 3:
                    pair, trio = first[source], rest[source]
                    last = pair[half]
                    own = pair[2 + half]
                    sixth = [trio[i] for i in range(6)]
                else:
                    last = first[3][half]
                    own = first[4][half]
                    sixth = [rest[3][i] for i in range(3)] + [rest[4][i] for i in range(3)]
                cbuf[:, 0:HD] = own
                for i in range(6):
                    lane = HD * (1 + i // 2)
                    low = (i % 2) * SUB
                    cbuf[low : low + SUB, lane : lane + HD] = sixth[i]
                cbuf[:, 4 * HD : 5 * HD] = last
                term = jnp.dot(cbuf[...], weights[source][...], preferred_element_type=f32)
                term = term.astype(bf16).astype(f32)
                total = term if total is None else total + term
            rows[half * HALF : (half + 1) * HALF, :] = total.astype(bf16)

    for sub in range(2):
        offset = offs_ref[step * 2 + sub]
        start = window_start(offset)
        onehot = slot_onehot(depth_ref[sub], offset - start)
        spread = lax.dot_general(
            onehot,
            rows[pl.ds(start, WINDOW), :],
            (((0,), (0,)), ((), ())),
            preferred_element_type=f32,
        )
        out[sub * TOK_BLOCK : (sub + 1) * TOK_BLOCK, :] = spread.astype(bf16)


def output_update(offsets, depth_blocks, groups, weights, length):
    width = weights[0].shape[1]
    steps = length // (2 * TOK_BLOCK)

    def whole(array):
        rank = array.ndim
        return pl.BlockSpec(array.shape, lambda i, o: (0,) * rank)

    return pl.pallas_call(
        output_kernel,
        out_shape=jax.ShapeDtypeStruct((length, width), bf16),
        grid_spec=pltpu.PrefetchScalarGridSpec(
            num_scalar_prefetch=1,
            grid=(steps,),
            in_specs=[pl.BlockSpec((2, 1, TOK_BLOCK), lambda i, o: (i, 0, 0))]
            + [whole(a) for a in groups]
            + [whole(a) for a in weights],
            out_specs=pl.BlockSpec((2 * TOK_BLOCK, width), lambda i, o: (i, 0)),
            scratch_shapes=[
                pltpu.VMEM((HALF, 5 * HD), bf16),
                pltpu.VMEM((ROOM, width), bf16),
            ],
        ),
        compiler_params=params(),
        name="output",
    )(offsets, depth_blocks, *groups, *weights)


def shift(value, axis, distance):
    size = lax.axis_size(axis)
    return lax.ppermute(value, axis, [(i, (i + distance) % size) for i in range(size)])


def ring_gather(value):
    middle = value.shape[0] // 2
    left = shift(value, "tensor", 1)
    right = shift(value, "tensor", -1)
    far_low = shift(left[:middle], "tensor", 1)
    far_high = shift(right[middle:], "tensor", -1)
    return [value, left, right, far_low, far_high]


def per_device(hidden, depth, qkv_weight, out_weight):
    tokens = hidden[0]
    length, width = tokens.shape
    t = lax.axis_index("tensor")
    ctx = lax.axis_index("ctx")
    depth_blocks = depth.reshape(length // TOK_BLOCK, 1, TOK_BLOCK)
    block_counts = jnp.sum((depth_blocks[:, 0] >= RECURSION).astype(jnp.int32), axis=1)
    order = jnp.arange(length // TOK_BLOCK)
    offsets = jnp.sum(
        jnp.where(order[:, None] > order[None, :], block_counts[None, :], 0), axis=1
    ).astype(jnp.int32)
    count = jnp.sum(block_counts).reshape(1)
    counts = jnp.concatenate([count] + [shift(count, "ctx", s) for s in (1, 2, 3)])
    place_ctx = jnp.concatenate([ctx.reshape(1).astype(jnp.int32), counts])
    place_both = jnp.stack([t, ctx]).astype(jnp.int32)

    rows = compact_rows(tokens, depth_blocks, offsets)
    weight = qkv_weight.reshape(qkv_weight.shape[0], -1)
    projected = []
    for half in range(2):
        own = rows[2 * half : 2 * half + 2]
        left = [shift(x, "tensor", 1) for x in own]
        right = [shift(x, "tensor", -1) for x in own]
        far = [shift(left[0], "tensor", 1), shift(right[1], "tensor", -1)]
        projected.append(project(place_both, own, left, right, far, weight))
    gathered = [lax.all_gather(p[5], "ctx", axis=0) for p in projected]
    arrived = []
    for s in range(4):
        for half in range(2):
            piece = projected[half][s]
            arrived.append(piece if s == 0 else shift(piece, "ctx", s))
    main = attend_main(place_ctx, arrived)
    last = attend_last(place_ctx, [p[4] for p in projected], gathered)
    returned = [[main[half]] for half in range(2)]
    for s in range(1, 4):
        for half in range(2):
            returned[half].append(shift(main[2 * s + half], "ctx", -s))
    groups = ring_gather(jnp.stack([last[0], last[1], main[0], main[1]]))
    for half in range(2):
        trio = jnp.stack(returned[half][1:]).reshape(6, SUB, HD)
        groups += ring_gather(trio)

    lower = out_weight[: 4 * HD]
    turned = lax.dynamic_slice_in_dim(jnp.concatenate([lower, lower]), ctx * HD, 4 * HD)
    arranged = jnp.concatenate([turned, out_weight[4 * HD :]])
    weights = []
    for distance in (0, 1, 3, 2):
        block = lax.dynamic_slice_in_dim(arranged, ((t + distance) & 3) * width, width, axis=1)
        weights.append(block if distance == 0 else shift(block, "tensor", distance))
    update = output_update(offsets, depth_blocks, groups, weights, length)
    return update[None]


def solution(mesh):
    placed = (P("dp", "ctx", "tensor"), P("dp", "ctx"), P(None, None, "tensor"), P("tensor", None))
    return jax.shard_map(
        per_device, mesh=mesh, in_specs=placed, out_specs=P("dp", "ctx", "tensor"), check_vma=False
    )
```

time: 563 us -> 326 us (0.58)
  waiting for transfers between devices: 208 us -> 100 us
  local copies, waits for them, and re-layouts: 139 us -> 38.8 us
  Pallas kernels: 0 us -> 83.5 us
  matrix products: 81.8 us -> 0 us
  other arithmetic: 53.5 us -> 9.8 us
  starting transfers between devices: 38.8 us -> 73.2 us
  blocking collectives: 16.9 us -> 0 us
    ppermute x0 -> x42, waiting for transfers between devices: none -> 100 us  [shift(): lax.ppermute(value, axis, [(i, (i + distance) % size) for i in range(size)])]
    all_gather x2, waiting for transfers between devices: 90.4 us -> 0.01 us  [per_device(): gathered = [lax.all_gather(p[5], 'ctx', axis=0) for p in projected]]
    pallas_call x0 -> x6, Pallas kernels: none -> 83.5 us  [the longest x2 27.1 us: project(): pl.pallas_call(project_kernel, out_shape=(stacked,) * 4 + (jax.ShapeDtype...]
    dot_general x4 -> x0, matrix products: 81.8 us -> none  [the longest x1 36.3 us: per_device(): jnp.einsum('qhd,khd->hqk', query_heads, key_heads, preferred_element_type...]
    ppermute x0 -> x42, starting transfers between devices: none -> 73.1 us  [shift(): lax.ppermute(value, axis, [(i, (i + distance) % size) for i in range(size)])]
    all_to_all x2 -> x0, waiting for transfers between devices: 60.6 us -> none  [move_tiles(): lax.all_to_all(payload, ('dp', 'ctx'), split_axis=0, concat_axis=0, tiled...]
    unnamed x4 -> x2, waiting for transfers between devices: 56.9 us -> 0.03 us
    all_to_all x2 -> x0, starting transfers between devices: 38.7 us -> none  [move_tiles(): lax.all_to_all(payload, ('dp', 'ctx'), split_axis=0, concat_axis=0, tiled...]
  transfers between devices with their start and end apart: 5 -> 44, of which waited for: 5 -> 18; matrix products, arithmetic and copies ran while one was open for 9% -> 13% of each run, Pallas kernels for 0% -> 13%
where the time goes in v1:
time: 326 us; the launch traced here: 320 us
  waiting for transfers between devices  100 us (31%)
  Pallas kernels  83.5 us (26%)
  starting transfers between devices  73.2 us (22%)
  local copies, waits for them, and re-layouts  38.8 us (12%)
  between operations  13.9 us (4%)
  other arithmetic  9.8 us (3%)
    ppermute x42, waiting for transfers between devices, shift(): lax.ppermute(value, axis, [(i, (i + distance) % size) for i in range(size)])  100 us
    ppermute x42, starting transfers between devices, shift(): lax.ppermute(value, axis, [(i, (i + distance) % size) for i in range(size)])  73.1 us
    pallas_call x2, Pallas kernels, project(): pl.pallas_call(project_kernel, out_shape=(stacked,) * 4 + (jax.ShapeDtype...  27.1 us
    pallas_call x1, Pallas kernels, attend_main(): pl.pallas_call(attend_main_kernel, out_shape=(jax.ShapeDtypeStruct((HALF,...  23.8 us
    unnamed x79, local copies, waits for them, and re-layouts  19.5 us
    pallas_call x1, Pallas kernels, output_update(): pl.pallas_call(output_kernel, out_shape=jax.ShapeDtypeStruct((length, wid...  17.8 us
    reshape x1, local copies, waits for them, and re-layouts, per_device(): weight = qkv_weight.reshape(qkv_weight.shape[0], -1)  14.4 us
    pallas_call x1, Pallas kernels, compact_rows(): pl.pallas_call(compact_kernel, out_shape=(sub,) * 4, grid_spec=pltpu.Pref...  10.4 us
  transfers between devices with their start and end apart: 44, of which 18 were waited for; matrix products, arithmetic and copies ran while one was open for 13% of the time, Pallas kernels for 13%

profile of v1, /device:TPU:1, one launch (start us, length us, event | category | flops | bytes accessed | tf_op | source)
XLA Modules:
  0.0 319.6 jit_solution(16394876584296694211)
XLA Ops:
  8.8 10.4 %compact.1 = (bf16[256,640]{1,0:T(8,128)(2,1)}, bf16[256,640]{1,0:T(8,128)(2,1)}, bf16[256,640]{1,0:T(8,128)(2,1)}, bf16[256,640]{1,0:T(8,128)(2,1)}) custom-call(s32[16]{0:T(128)} %select_reduce_fusion.offs_ref, s32[16,1,256]{2,1,0:T(1,128)} %bitcast.31, bf16[4096,640]{1,0:T(8,128)(2,1)} %bitcast.22), custom_call_target="tpu_custom_call" | custom-call | tf_op jit(solution)/shard_map/compact/pallas_call | solution.py:77
  23.8 2.7 collective-permute-start.5
  26.4 5.0 %collective-permute-done.3.a0 = bf16[256,640]{1,0:T(8,128)(2,1)S(1)} collective-permute-done((bf16[256,640]{1,0:T(8,128)(2,1)}, bf16[256,640]{1,0:T(8,128)(2,1)S(1)}, u32[]{:S(2)}, u32[]{:S(2)}) %collective-permute-start.3) | collective-permute-done | bytes 327712 | tf_op jit(solution)/shard_map/ppermute | solution.py:381
  31.4 2.7 collective-permute-start.8
  34.1 13.8 %copy.12 = bf16[2560,3,640]{0,2,1:T(8,128)(2,1)} copy(bf16[2560,3,640]{2,0,1:T(8,128)(2,1)} %param.6) | data formatting | bytes 19660800 | tf_op args[2]
  47.9 14.4 %copy.13.w_ref = bf16[2560,1920]{1,0:T(8,128)(2,1)} copy(bf16[2560,1920]{0,1:T(8,128)(2,1)} %bitcast.21) | data formatting | bytes 19660800 | tf_op jit(solution)/shard_map/reshape | solution.py:410
  64.6 13.6 %project.2 = (bf16[3,512,128]{2,1,0:T(8,128)(2,1)}, bf16[3,512,128]{2,1,0:T(8,128)(2,1)}, bf16[3,512,128]{2,1,0:T(8,128)(2,1)}, bf16[3,512,128]{2,1,0:T(8,128)(2...) custom-call(s32[2]{0:T(128)} %pad_add_fusion.place, bf16[256,640]{1,0:T(8,128)(2,1)} %get-tuple-element.31.x0, ...), custom_call_target="tpu_custom_call" | custom-call | tf_op jit(solution)/shard_map/project/pallas_call | solution.py:144
  78.4 2.7 collective-permute-start.12
  81.0 2.7 collective-permute-start.11
  83.7 2.6 collective-permute-done.9.a0
  86.3 2.7 collective-permute-start.14
  89.0 4.3 %collective-permute-done.10.a1 = bf16[256,640]{1,0:T(8,128)(2,1)S(1)} collective-permute-done((bf16[256,640]{1,0:T(8,128)(2,1)}, bf16[256,640]{1,0:T(8,128)(2,1)S(1)}, u32[]{:S(2)}, u32[]{:S(2)}) %collective-permute-start.10) | collective-permute-done | bytes 327712 | tf_op jit(solution)/shard_map/ppermute | solution.py:381
  93.3 7.1 %collective-permute-done.13.c0 = bf16[256,640]{1,0:T(8,128)(2,1)S(1)} collective-permute-done((bf16[256,640]{1,0:T(8,128)(2,1)S(1)}, bf16[256,640]{1,0:T(8,128)(2,1)S(1)}, u32[]{:S(2)}, u32[]{:S(2)}) %collective-permute-start.13) | collective-permute-done | bytes 327712 | tf_op jit(solution)/shard_map/ppermute | solution.py:381
  101.9 13.5 %project.3 = (bf16[3,512,128]{2,1,0:T(8,128)(2,1)}, bf16[3,512,128]{2,1,0:T(8,128)(2,1)}, bf16[3,512,128]{2,1,0:T(8,128)(2,1)}, bf16[3,512,128]{2,1,0:T(8,128)(2...) custom-call(s32[2]{0:T(128)} %pad_add_fusion.place, bf16[256,640]{1,0:T(8,128)(2,1)} %get-tuple-element.34.x0, ...), custom_call_target="tpu_custom_call" | custom-call | tf_op jit(solution)/shard_map/project/pallas_call | solution.py:144
  119.6 3.8 %fusion = bf16[512,2560]{1,0:T(8,128)(2,1)S(1)} fusion(s32[]{:T(128)S(6)} %select_n.20, bf16[512,2560]{1,0:T(8,128)(2,1)} %slice.30), kind=kLoop, calls=%fused_computation.10 | loop fusion | flops 5242880 | bytes 5242884 | tf_op jit(solution)/shard_map/concatenate | solution.py:436
  127.9 8.0 %collective-permute-done = s32[1]{0:T(128)} collective-permute-done((s32[1]{0:T(128)}, s32[1]{0:T(128)}, u32[]{:S(2)}, u32[]{:S(2)}) %collective-permute-start) | collective-permute-done | bytes 36 | tf_op jit(solution)/shard_map/ppermute | solution.py:381
  142.2 3.2 concatenate.9.place
  145.3 6.4 %collective-permute-done.17.refs_4_ = bf16[3,512,128]{2,1,0:T(8,128)(2,1)S(1)} collective-permute-done((bf16[3,512,128]{2,1,0:T(8,128)(2,1)}, bf16[3,512,128]{2,1,0:T(8,128)(2,1)S(1)}, u32[]{:S(2)}, u32[]{:S(2)}) %collective-permute-start.17) | collective-permute-done | bytes 393248 | tf_op jit(solution)/shard_map/ppermute | solution.py:381
  151.7 4.2 %collective-permute-done.18.refs_5_ = bf16[3,512,128]{2,1,0:T(8,128)(2,1)S(1)} collective-permute-done((bf16[3,512,128]{2,1,0:T(8,128)(2,1)}, bf16[3,512,128]{2,1,0:T(8,128)(2,1)S(1)}, u32[]{:S(2)}, u32[]{:S(2)}) %collective-permute-start.18) | collective-permute-done | bytes 393248 | tf_op jit(solution)/shard_map/ppermute | solution.py:381
  156.0 3.7 %collective-permute-done.20.refs_7_ = bf16[3,512,128]{2,1,0:T(8,128)(2,1)S(1)} collective-permute-done((bf16[3,512,128]{2,1,0:T(8,128)(2,1)}, bf16[3,512,128]{2,1,0:T(8,128)(2,1)S(1)}, u32[]{:S(2)}, u32[]{:S(2)}) %collective-permute-start.20) | collective-permute-done | bytes 393248 | tf_op jit(solution)/shard_map/ppermute | solution.py:381
  160.4 23.8 %attend_main.1 = (bf16[512,128]{1,0:T(8,128)(2,1)}, bf16[512,128]{1,0:T(8,128)(2,1)}, bf16[512,128]{1,0:T(8,128)(2,1)}, bf16[512,128]{1,0:T(8,128)(2,1)}, bf16[5...) custom-call(s32[5]{0:T(128)} %concatenate.9.place, ...), custom_call_target="tpu_custom_call" | custom-call | tf_op jit(solution)/shard_map/attend_main/pallas_call | solution.py:244
  192.7 12.3 %collective-permute-start.28 = (bf16[6,256,128]{2,1,0:T(8,128)(2,1)S(1)}, bf16[6,256,128]{2,1,0:T(8,128)(2,1)S(1)}, u32[]{:S(2)}, u32[]{:S(2)}) collective-permute-start(bf16[6,256,128]{2,1,0:T(8,128)(2,1)S(1)} %bitcast.23), channel_id=1, source_target_pairs={{0,1},{1,2},{2,3},{3,0},{4,5},{5,6},{6,7},{7,4},{8,9},{9,10},{10,1... | collective-permute-start | bytes 1179656 | tf_op jit(solution)/shard_map/ppermute | solution.py:381
  205.9 4.4 %attend_last.1 = (bf16[512,128]{1,0:T(8,128)(2,1)}, bf16[512,128]{1,0:T(8,128)(2,1)}) custom-call(s32[5]{0:T(128)} %concatenate.9.place, bf16[512,128]{1,0:T(8,128)(2,1)} %get-tuple-element.33.q0, bf16[512,128]{1,0:T(8,128)(2,1)} %get-tuple-element.36.q1, bf16[4,2,512,128]{3,2,1,0:T(8,128)(2,1)} %bitcast.29, bf16[4,2,512,128]{3,2,1,0:T(8,128)(2,1)} %bitcast.30), custom_call_target="tpu_custom_call" | custom-call | tf_op jit(solution)/shard_map/attend_last/pallas_call | solution.py:291
  212.3 6.8 %collective-permute-start.33 = (bf16[512,128]{1,0:T(8,128)(2,1)S(1)}, bf16[512,128]{1,0:T(8,128)(2,1)S(1)}, u32[]{:S(2)}, u32[]{:S(2)}) collective-permute-start(bf16[512,128]{1,0:T(8,128)(2,1)S(1)} %copy-done.38), channel_id=1, source_target_pairs={{0,8},{4,12},{8,0},{12,4},{1,9},{5,13},{9,1},{13,5},{2,10},{6,14},... | collective-permute-start | bytes 393224 | tf_op jit(solution)/shard_map/ppermute | solution.py:381
  223.2 2.8 collective-permute-done.32
  228.6 4.1 %collective-permute-done.29.refs_7_ = bf16[6,256,128]{2,1,0:T(8,128)(2,1)S(1)} collective-permute-done((bf16[6,256,128]{2,1,0:T(8,128)(2,1)S(1)}, bf16[6,256,128]{2,1,0:T(8,128)(2,1)S(1)}, u32[]{:S(2)}, u32[]{:S(2)}) %collective-permute-start.29) | collective-permute-done | bytes 393248 | tf_op jit(solution)/shard_map/ppermute | solution.py:381
  232.8 2.8 collective-permute-start.36
  235.6 40.1 %collective-permute-done.22.refs_2_ = bf16[4,512,128]{2,1,0:T(8,128)(2,1)S(1)} collective-permute-done((bf16[4,512,128]{2,1,0:T(8,128)(2,1)S(1)}, bf16[4,512,128]{2,1,0:T(8,128)(2,1)S(1)}, u32[]{:S(2)}, u32[]{:S(2)}) %collective-permute-start.22) | collective-permute-done | bytes 524320 | tf_op jit(solution)/shard_map/ppermute | solution.py:381
  277.6 4.7 %collective-permute-done.36.refs_12_ = bf16[6,256,128]{2,1,0:T(8,128)(2,1)S(1)} collective-permute-done((bf16[6,256,128]{2,1,0:T(8,128)(2,1)S(1)}, bf16[6,256,128]{2,1,0:T(8,128)(2,1)S(1)}, u32[]{:S(2)}, u32[]{:S(2)}) %collective-permute-start.36) | collective-permute-done | bytes 393248 | tf_op jit(solution)/shard_map/ppermute | solution.py:381
  282.2 3.2 %collective-permute-start.24 = (bf16[2,512,128]{2,1,0:T(8,128)(2,1)S(1)}, bf16[2,512,128]{2,1,0:T(8,128)(2,1)S(1)}, u32[]{:S(2)}, u32[]{:S(2)}) collective-permute-start(bf16[2,512,128]{2,1,0:T(8,128)(2,1)S(1)} %slice.33), channel_id=1, source_target_pairs={{0,3},{1,0},{2,1},{3,2},{4,7},{5,4},{6,5},{7,6},{8,11},{9,8},{10,9... | collective-permute-start | bytes 786440 | tf_op jit(solution)/shard_map/ppermute | solution.py:381
  289.3 2.6 collective-permute-done.31.refs_9_
  294.9 17.8 %output.1 = bf16[4096,640]{1,0:T(8,128)(2,1)} custom-call(s32[16]{0:T(128)} %select_reduce_fusion.offs_ref, s32[16,1,256]{2,1,0:T(1,128)} %bitcast.32, bf16[4,512,128]{2,1,0:T(8,128)(2,1)} %copy-done.1, bf16[4,512,128]{2,1,0:T(8,128)(2,1)} %copy-done.4, bf16[4,512,128]{2,1,0:T(8,128)(2,1)} %copy-done.5, bf16[2,512,128]{2,1,0:T(8,128)(2,1)} %copy-done.31, ...), custom_call_target="tpu_custom_call" | custom-call | tf_op jit(solution)/shard_map/output/pallas_call | solution.py:359
  (164 shorter events, 53.2 us)
Async XLA Ops:
  6.5 199.4 %all-gather.5.cloned.1.call-start = ((), (), s32[]{:S(2)}) async-start(), calls=%async_computation | async-start | bytes 1310720 | tf_op jit(solution)/shard_map/all_gather | solution.py:418
  19.2 12.2 %collective-permute-start.3 = (bf16[256,640]{1,0:T(8,128)(2,1)}, bf16[256,640]{1,0:T(8,128)(2,1)S(1)}, u32[]{:S(2)}, u32[]{:S(2)}) collective-permute-start(bf16[256,640]{1,0:T(8,128)(2,1)} %get-tuple-element.31.x0), channel_id=1, source_target_pairs={{0,1},{1,2},{2,3},{3,0},{4,5},{5,6},{6,7},{7,4},{8,9},{9,10},{10,1... | collective-permute-start | bytes 983048 | tf_op jit(solution)/shard_map/ppermute | solution.py:381
  23.8 39.1 %collective-permute-start.4 = (bf16[256,640]{1,0:T(8,128)(2,1)}, bf16[256,640]{1,0:T(8,128)(2,1)S(1)}, u32[]{:S(2)}, u32[]{:S(2)}) collective-permute-start(bf16[256,640]{1,0:T(8,128)(2,1)} %get-tuple-element.32.x1), channel_id=1, source_target_pairs={{0,1},{1,2},{2,3},{3,0},{4,5},{5,6},{6,7},{7,4},{8,9},{9,10},{10,1... | collective-permute-start | bytes 983048 | tf_op jit(solution)/shard_map/ppermute | solution.py:381
  23.8 39.2 %collective-permute-start.5 = (bf16[256,640]{1,0:T(8,128)(2,1)}, bf16[256,640]{1,0:T(8,128)(2,1)S(1)}, u32[]{:S(2)}, u32[]{:S(2)}) collective-permute-start(bf16[256,640]{1,0:T(8,128)(2,1)} %get-tuple-element.31.x0), channel_id=1, source_target_pairs={{0,3},{1,0},{2,1},{3,2},{4,7},{5,4},{6,5},{7,6},{8,11},{9,8},{10,9... | collective-permute-start | bytes 983048 | tf_op jit(solution)/shard_map/ppermute | solution.py:381
  31.4 31.5 %collective-permute-start.7 = (bf16[256,640]{1,0:T(8,128)(2,1)S(1)}, bf16[256,640]{1,0:T(8,128)(2,1)S(1)}, u32[]{:S(2)}, u32[]{:S(2)}) collective-permute-start(bf16[256,640]{1,0:T(8,128)(2,1)S(1)} %collective-permute-done.3.a0), channel_id=1, source_target_pairs={{0,1},{1,2},{2,3},{3,0},{4,5},{5,6},{6,7},{7,4},{8,9},{9,10},{10,1... | collective-permute-start | bytes 983048 | tf_op jit(solution)/shard_map/ppermute | solution.py:381
  31.4 31.5 %collective-permute-start.8 = (bf16[256,640]{1,0:T(8,128)(2,1)S(1)}, bf16[256,640]{1,0:T(8,128)(2,1)S(1)}, u32[]{:S(2)}, u32[]{:S(2)}) collective-permute-start(bf16[256,640]{1,0:T(8,128)(2,1)S(1)} %collective-permute-done.6.b1), channel_id=1, source_target_pairs={{0,3},{1,0},{2,1},{3,2},{4,7},{5,4},{6,5},{7,6},{8,11},{9,8},{10,9... | collective-permute-start | bytes 983048 | tf_op jit(solution)/shard_map/ppermute | solution.py:381
  78.2 127.7 %all-gather.7.cloned.1.call-start = ((), (), s32[]{:S(2)}) async-start(), calls=%async_computation.1 | async-start | bytes 1310720 | tf_op jit(solution)/shard_map/all_gather | solution.py:418
  81.0 12.3 %collective-permute-start.10 = (bf16[256,640]{1,0:T(8,128)(2,1)}, bf16[256,640]{1,0:T(8,128)(2,1)S(1)}, u32[]{:S(2)}, u32[]{:S(2)}) collective-permute-start(bf16[256,640]{1,0:T(8,128)(2,1)} %get-tuple-element.35.x1), channel_id=1, source_target_pairs={{0,1},{1,2},{2,3},{3,0},{4,5},{5,6},{6,7},{7,4},{8,9},{9,10},{10,1... | collective-permute-start | bytes 983048 | tf_op jit(solution)/shard_map/ppermute | solution.py:381
  81.0 12.3 %collective-permute-start.11 = (bf16[256,640]{1,0:T(8,128)(2,1)}, bf16[256,640]{1,0:T(8,128)(2,1)S(1)}, u32[]{:S(2)}, u32[]{:S(2)}) collective-permute-start(bf16[256,640]{1,0:T(8,128)(2,1)} %get-tuple-element.34.x0), channel_id=1, source_target_pairs={{0,3},{1,0},{2,1},{3,2},{4,7},{5,4},{6,5},{7,6},{8,11},{9,8},{10,9... | collective-permute-start | bytes 983048 | tf_op jit(solution)/shard_map/ppermute | solution.py:381
  86.3 14.1 %collective-permute-start.13 = (bf16[256,640]{1,0:T(8,128)(2,1)S(1)}, bf16[256,640]{1,0:T(8,128)(2,1)S(1)}, u32[]{:S(2)}, u32[]{:S(2)}) collective-permute-start(bf16[256,640]{1,0:T(8,128)(2,1)S(1)} %collective-permute-done.9.a0), channel_id=1, source_target_pairs={{0,1},{1,2},{2,3},{3,0},{4,5},{5,6},{6,7},{7,4},{8,9},{9,10},{10,1... | collective-permute-start | bytes 983048 | tf_op jit(solution)/shard_map/ppermute | solution.py:381
  86.3 14.1 %collective-permute-start.14 = (bf16[256,640]{1,0:T(8,128)(2,1)S(1)}, bf16[256,640]{1,0:T(8,128)(2,1)S(1)}, u32[]{:S(2)}, u32[]{:S(2)}) collective-permute-start(bf16[256,640]{1,0:T(8,128)(2,1)S(1)} %collective-permute-done.12.b1), channel_id=1, source_target_pairs={{0,3},{1,0},{2,1},{3,2},{4,7},{5,4},{6,5},{7,6},{8,11},{9,8},{10,9... | collective-permute-start | bytes 983048 | tf_op jit(solution)/shard_map/ppermute | solution.py:381
  117.1 23.9 %collective-permute-start.15 = (bf16[3,512,128]{2,1,0:T(8,128)(2,1)}, bf16[3,512,128]{2,1,0:T(8,128)(2,1)}, u32[]{:S(2)}, u32[]{:S(2)}) collective-permute-start(bf16[3,512,128]{2,1,0:T(8,128)(2,1)} %get-tuple-element.43), channel_id=1, source_target_pairs={{0,4},{4,8},{8,12},{12,0},{1,5},{5,9},{9,13},{13,1},{2,6},{6,10},{... | collective-permute-start | bytes 1179656 | tf_op jit(solution)/shard_map/ppermute | solution.py:381
  118.3 23.8 %collective-permute-start.16 = (bf16[3,512,128]{2,1,0:T(8,128)(2,1)}, bf16[3,512,128]{2,1,0:T(8,128)(2,1)}, u32[]{:S(2)}, u32[]{:S(2)}) collective-permute-start(bf16[3,512,128]{2,1,0:T(8,128)(2,1)} %get-tuple-element.44), channel_id=1, source_target_pairs={{0,4},{4,8},{8,12},{12,0},{1,5},{5,9},{9,13},{13,1},{2,6},{6,10},{... | collective-permute-start | bytes 1179656 | tf_op jit(solution)/shard_map/ppermute | solution.py:381
  125.3 93.8 %collective-permute-start.39 = (bf16[640,640]{1,0:T(8,128)(2,1)}, bf16[640,640]{1,0:T(8,128)(2,1)S(1)}, u32[]{:S(2)}, u32[]{:S(2)}) collective-permute-start(bf16[640,640]{1,0:T(8,128)(2,1)} %get-tuple-element.61), channel_id=1, source_target_pairs={{0,1},{1,2},{2,3},{3,0},{4,5},{5,6},{6,7},{7,4},{8,9},{9,10},{10,1... | collective-permute-start | bytes 2457608 | tf_op jit(solution)/shard_map/ppermute | solution.py:381
  126.3 11.7 %collective-permute-start.1 = (s32[1]{0:T(128)}, s32[1]{0:T(128)}, u32[]{:S(2)}, u32[]{:S(2)}) collective-permute-start(s32[1]{0:T(128)} %bitcast.2), channel_id=1, source_target_pairs={{0,8},{4,12},{8,0},{12,4},{1,9},{5,13},{9,1},{13,5},{2,10},{6,14},... | collective-permute-start | bytes 20 | tf_op jit(solution)/shard_map/ppermute | solution.py:381
  138.1 13.7 %collective-permute-start.17 = (bf16[3,512,128]{2,1,0:T(8,128)(2,1)}, bf16[3,512,128]{2,1,0:T(8,128)(2,1)S(1)}, u32[]{:S(2)}, u32[]{:S(2)}) collective-permute-start(bf16[3,512,128]{2,1,0:T(8,128)(2,1)} %get-tuple-element.45), channel_id=1, source_target_pairs={{0,8},{4,12},{8,0},{12,4},{1,9},{5,13},{9,1},{13,5},{2,10},{6,14},... | collective-permute-start | bytes 1179656 | tf_op jit(solution)/shard_map/ppermute | solution.py:381
  138.8 17.1 %collective-permute-start.18 = (bf16[3,512,128]{2,1,0:T(8,128)(2,1)}, bf16[3,512,128]{2,1,0:T(8,128)(2,1)S(1)}, u32[]{:S(2)}, u32[]{:S(2)}) collective-permute-start(bf16[3,512,128]{2,1,0:T(8,128)(2,1)} %get-tuple-element.46), channel_id=1, source_target_pairs={{0,8},{4,12},{8,0},{12,4},{1,9},{5,13},{9,1},{13,5},{2,10},{6,14},... | collective-permute-start | bytes 1179656 | tf_op jit(solution)/shard_map/ppermute | solution.py:381
  141.0 14.9 %collective-permute-start.19 = (bf16[3,512,128]{2,1,0:T(8,128)(2,1)}, bf16[3,512,128]{2,1,0:T(8,128)(2,1)S(1)}, u32[]{:S(2)}, u32[]{:S(2)}) collective-permute-start(bf16[3,512,128]{2,1,0:T(8,128)(2,1)} %get-tuple-element.47), channel_id=1, source_target_pairs={{0,12},{4,0},{8,4},{12,8},{1,13},{5,1},{9,5},{13,9},{2,14},{6,2},{... | collective-permute-start | bytes 1179656 | tf_op jit(solution)/shard_map/ppermute | solution.py:381
  142.1 17.5 %collective-permute-start.20 = (bf16[3,512,128]{2,1,0:T(8,128)(2,1)}, bf16[3,512,128]{2,1,0:T(8,128)(2,1)S(1)}, u32[]{:S(2)}, u32[]{:S(2)}) collective-permute-start(bf16[3,512,128]{2,1,0:T(8,128)(2,1)} %get-tuple-element.48), channel_id=1, source_target_pairs={{0,12},{4,0},{8,4},{12,8},{1,13},{5,1},{9,5},{13,9},{2,14},{6,2},{... | collective-permute-start | bytes 1179656 | tf_op jit(solution)/shard_map/ppermute | solution.py:381
  192.7 33.8 %collective-permute-start.28 = (bf16[6,256,128]{2,1,0:T(8,128)(2,1)S(1)}, bf16[6,256,128]{2,1,0:T(8,128)(2,1)S(1)}, u32[]{:S(2)}, u32[]{:S(2)}) collective-permute-start(bf16[6,256,128]{2,1,0:T(8,128)(2,1)S(1)} %bitcast.23), channel_id=1, source_target_pairs={{0,1},{1,2},{2,3},{3,0},{4,5},{5,6},{6,7},{7,4},{8,9},{9,10},{10,1... | collective-permute-start | bytes 1179656 | tf_op jit(solution)/shard_map/ppermute | solution.py:381
  205.0 16.4 %collective-permute-start.34 = (bf16[512,128]{1,0:T(8,128)(2,1)}, bf16[512,128]{1,0:T(8,128)(2,1)S(1)}, u32[]{:S(2)}, u32[]{:S(2)}) collective-permute-start(bf16[512,128]{1,0:T(8,128)(2,1)} %get-tuple-element.56), channel_id=1, source_target_pairs={{0,4},{4,8},{8,12},{12,0},{1,5},{5,9},{9,13},{13,1},{2,6},{6,10},{... | collective-permute-start | bytes 393224 | tf_op jit(solution)/shard_map/ppermute | solution.py:381
  211.4 21.3 %collective-permute-start.21 = (bf16[4,512,128]{2,1,0:T(8,128)(2,1)S(1)}, bf16[4,512,128]{2,1,0:T(8,128)(2,1)S(1)}, u32[]{:S(2)}, u32[]{:S(2)}) collective-permute-start(bf16[4,512,128]{2,1,0:T(8,128)(2,1)S(1)} %pad_maximum_fusion.refs_0_), channel_id=1, source_target_pairs={{0,1},{1,2},{2,3},{3,0},{4,5},{5,6},{6,7},{7,4},{8,9},{9,10},{10,1... | collective-permute-start | bytes 1572872 | tf_op jit(solution)/shard_map/ppermute | solution.py:381
  212.3 10.8 %collective-permute-start.33 = (bf16[512,128]{1,0:T(8,128)(2,1)S(1)}, bf16[512,128]{1,0:T(8,128)(2,1)S(1)}, u32[]{:S(2)}, u32[]{:S(2)}) collective-permute-start(bf16[512,128]{1,0:T(8,128)(2,1)S(1)} %copy-done.38), channel_id=1, source_target_pairs={{0,8},{4,12},{8,0},{12,4},{1,9},{5,13},{9,1},{13,5},{2,10},{6,14},... | collective-permute-start | bytes 393224 | tf_op jit(solution)/shard_map/ppermute | solution.py:381
  221.4 11.2 %collective-permute-start.29 = (bf16[6,256,128]{2,1,0:T(8,128)(2,1)S(1)}, bf16[6,256,128]{2,1,0:T(8,128)(2,1)S(1)}, u32[]{:S(2)}, u32[]{:S(2)}) collective-permute-start(bf16[6,256,128]{2,1,0:T(8,128)(2,1)S(1)} %bitcast.24), channel_id=1, source_target_pairs={{0,3},{1,0},{2,1},{3,2},{4,7},{5,4},{6,5},{7,6},{8,11},{9,8},{10,9... | collective-permute-start | bytes 1179656 | tf_op jit(solution)/shard_map/ppermute | solution.py:381
  223.1 62.4 %collective-permute-start.40 = (bf16[640,640]{1,0:T(8,128)(2,1)S(1)}, bf16[640,640]{1,0:T(8,128)(2,1)S(1)}, u32[]{:S(2)}, u32[]{:S(2)}) collective-permute-start(bf16[640,640]{1,0:T(8,128)(2,1)S(1)} %copy-done.11), channel_id=1, source_target_pairs={{0,3},{1,0},{2,1},{3,2},{4,7},{5,4},{6,5},{7,6},{8,11},{9,8},{10,9... | collective-permute-start | bytes 2457608 | tf_op jit(solution)/shard_map/ppermute | solution.py:381
  226.0 59.6 %collective-permute-start.41 = (bf16[640,640]{1,0:T(8,128)(2,1)S(1)}, bf16[640,640]{1,0:T(8,128)(2,1)S(1)}, u32[]{:S(2)}, u32[]{:S(2)}) collective-permute-start(bf16[640,640]{1,0:T(8,128)(2,1)S(1)} %copy-done.10), channel_id=1, source_target_pairs={{0,2},{1,3},{2,0},{3,1},{4,6},{5,7},{6,4},{7,5},{8,10},{9,11},{10,... | collective-permute-start | bytes 2457608 | tf_op jit(solution)/shard_map/ppermute | solution.py:381
  226.5 49.2 %collective-permute-start.22 = (bf16[4,512,128]{2,1,0:T(8,128)(2,1)S(1)}, bf16[4,512,128]{2,1,0:T(8,128)(2,1)S(1)}, u32[]{:S(2)}, u32[]{:S(2)}) collective-permute-start(bf16[4,512,128]{2,1,0:T(8,128)(2,1)S(1)} %pad_maximum_fusion.refs_0_), channel_id=1, source_target_pairs={{0,3},{1,0},{2,1},{3,2},{4,7},{5,4},{6,5},{7,6},{8,11},{9,8},{10,9... | collective-permute-start | bytes 1572872 | tf_op jit(solution)/shard_map/ppermute | solution.py:381
  232.6 44.8 %collective-permute-start.35 = (bf16[6,256,128]{2,1,0:T(8,128)(2,1)S(1)}, bf16[6,256,128]{2,1,0:T(8,128)(2,1)S(1)}, u32[]{:S(2)}, u32[]{:S(2)}) collective-permute-start(bf16[6,256,128]{2,1,0:T(8,128)(2,1)S(1)} %bitcast.26), channel_id=1, source_target_pairs={{0,1},{1,2},{2,3},{3,0},{4,5},{5,6},{6,7},{7,4},{8,9},{9,10},{10,1... | collective-permute-start | bytes 1179656 | tf_op jit(solution)/shard_map/ppermute | solution.py:381
  232.8 49.5 %collective-permute-start.36 = (bf16[6,256,128]{2,1,0:T(8,128)(2,1)S(1)}, bf16[6,256,128]{2,1,0:T(8,128)(2,1)S(1)}, u32[]{:S(2)}, u32[]{:S(2)}) collective-permute-start(bf16[6,256,128]{2,1,0:T(8,128)(2,1)S(1)} %bitcast.27), channel_id=1, source_target_pairs={{0,3},{1,0},{2,1},{3,2},{4,7},{5,4},{6,5},{7,6},{8,11},{9,8},{10,9... | collective-permute-start | bytes 1179656 | tf_op jit(solution)/shard_map/ppermute | solution.py:381
  275.7 12.3 %collective-permute-start.30 = (bf16[3,256,128]{2,1,0:T(8,128)(2,1)S(1)}, bf16[3,256,128]{2,1,0:T(8,128)(2,1)S(1)}, u32[]{:S(2)}, u32[]{:S(2)}) collective-permute-start(bf16[3,256,128]{2,1,0:T(8,128)(2,1)S(1)} %slice.34), channel_id=1, source_target_pairs={{0,1},{1,2},{2,3},{3,0},{4,5},{5,6},{6,7},{7,4},{8,9},{9,10},{10,1... | collective-permute-start | bytes 589832 | tf_op jit(solution)/shard_map/ppermute | solution.py:381
  277.5 16.5 %collective-permute-start.23 = (bf16[2,512,128]{2,1,0:T(8,128)(2,1)S(1)}, bf16[2,512,128]{2,1,0:T(8,128)(2,1)S(1)}, u32[]{:S(2)}, u32[]{:S(2)}) collective-permute-start(bf16[2,512,128]{2,1,0:T(8,128)(2,1)S(1)} %slice.32), channel_id=1, source_target_pairs={{0,1},{1,2},{2,3},{3,0},{4,5},{5,6},{6,7},{7,4},{8,9},{9,10},{10,1... | collective-permute-start | bytes 786440 | tf_op jit(solution)/shard_map/ppermute | solution.py:381
  282.2 11.7 %collective-permute-start.24 = (bf16[2,512,128]{2,1,0:T(8,128)(2,1)S(1)}, bf16[2,512,128]{2,1,0:T(8,128)(2,1)S(1)}, u32[]{:S(2)}, u32[]{:S(2)}) collective-permute-start(bf16[2,512,128]{2,1,0:T(8,128)(2,1)S(1)} %slice.33), channel_id=1, source_target_pairs={{0,3},{1,0},{2,1},{3,2},{4,7},{5,4},{6,5},{7,6},{8,11},{9,8},{10,9... | collective-permute-start | bytes 786440 | tf_op jit(solution)/shard_map/ppermute | solution.py:381
  (52 other events, 965.1 us)
Sparse Core Ops, SparseCore 0:
  78.3 24.2 all-gather.4
  115.6 35.3 all-gather.6

commit v2 on v1

v2 whole, which is shorter than its diff:
```python
import functools
import math

import jax
import jax.numpy as jnp
from jax import lax
from jax.experimental import pallas as pl
from jax.experimental.pallas import tpu as pltpu
from jax.sharding import PartitionSpec as P

HD = 128
RECURSION = 3
CAP = 1024
HALF = CAP // 2
SUB = CAP // 4
TOK_BLOCK = 256
WINDOW = 384
ROOM = CAP + WINDOW

score_scale = 0.25
norm_epsilon = 1e-05
head_epsilon = 1e-06
EXP2_SCALE = score_scale / math.log(2.0)
VMEM_LIMIT = 56 * 1024 * 1024

bf16 = jnp.bfloat16
f32 = jnp.float32


def cost(micros):
    return pl.CostEstimate(flops=int(micros * 1.1e9), bytes_accessed=0, transcendentals=0)


def params(**more):
    return pltpu.CompilerParams(vmem_limit_bytes=VMEM_LIMIT, **more)


def slot_onehot(depth_row, shift):
    active = depth_row >= RECURSION
    flags = jnp.broadcast_to(jnp.where(active, 1.0, 0.0), (8, TOK_BLOCK)).astype(bf16)
    before = lax.broadcasted_iota(jnp.int32, (TOK_BLOCK, TOK_BLOCK), 0)
    after = lax.broadcasted_iota(jnp.int32, (TOK_BLOCK, TOK_BLOCK), 1)
    earlier = jnp.where(before < after, 1.0, 0.0).astype(bf16)
    rank = jnp.dot(flags, earlier, preferred_element_type=f32)[0:1].astype(jnp.int32)
    slot = jnp.where(active, rank + shift, -1)
    rows = lax.broadcasted_iota(jnp.int32, (WINDOW, TOK_BLOCK), 0)
    return jnp.where(rows == slot, 1.0, 0.0).astype(bf16)


def window_start(offset):
    return pl.multiple_of((offset >> 7) << 7, 128)


def compact_kernel(offs_ref, depth_ref, tok_ref, o0, o1, buf):
    step = pl.program_id(0)

    @pl.when(step == 0)
    def _():
        buf[...] = jnp.zeros_like(buf)

    for sub in range(2):
        offset = offs_ref[step * 2 + sub]
        start = window_start(offset)
        onehot = slot_onehot(depth_ref[sub], offset - start)
        picked = jnp.dot(
            onehot,
            tok_ref[sub * TOK_BLOCK : (sub + 1) * TOK_BLOCK, :],
            preferred_element_type=f32,
        ).astype(bf16)
        buf[pl.ds(start, WINDOW), :] = buf[pl.ds(start, WINDOW), :] + picked

    @pl.when(step == pl.num_programs(0) - 1)
    def _():
        for i, o in enumerate((o0, o1)):
            o[...] = buf[i * HALF : (i + 1) * HALF, :]


def compact_rows(tokens, depth_blocks, offsets):
    length, width = tokens.shape
    steps = length // (2 * TOK_BLOCK)
    return pl.pallas_call(
        compact_kernel,
        out_shape=(jax.ShapeDtypeStruct((HALF, width), bf16),) * 2,
        grid_spec=pltpu.PrefetchScalarGridSpec(
            num_scalar_prefetch=1,
            grid=(steps,),
            in_specs=[
                pl.BlockSpec((2, 1, TOK_BLOCK), lambda i, o: (i, 0, 0)),
                pl.BlockSpec((2 * TOK_BLOCK, width), lambda i, o: (i, 0)),
            ],
            out_specs=(pl.BlockSpec((HALF, width), lambda i, o: (0, 0)),) * 2,
            scratch_shapes=[pltpu.VMEM((ROOM, width), bf16)],
        ),
        compiler_params=params(),
        cost_estimate=cost(8),
        name="compact",
    )(offsets, depth_blocks, tokens)


def project_kernel(place, x, a, b, c, d, w_ref, o0, o1, o2, o3, q4, xs, acc):
    part = pl.program_id(0)
    t = place[0]
    ctx = place[1]
    width = x.shape[1]

    @pl.when(part == 0)
    def _():
        for sub, far in enumerate((c, d)):
            low = sub * SUB
            pieces = [p[low : low + SUB, :] for p in (x, a, b)] + [far[...]]
            squares = jnp.zeros((SUB, 1), f32)
            for piece in pieces:
                wide = piece.astype(f32)
                squares = squares + jnp.sum(wide * wide, axis=1, keepdims=True)
            factor = lax.rsqrt(squares * (1.0 / (4 * width)) + norm_epsilon)
            for distance, piece in zip((0, 3, 1, 2), pieces):
                lane = pl.multiple_of(((t + distance) & 3) * width, 128)
                normed = (piece.astype(f32) * factor).astype(bf16)
                xs[low : low + SUB, pl.ds(lane, width)] = normed

    acc[...] = jnp.dot(xs[...], w_ref[0], preferred_element_type=f32)

    def column(y):
        scale = lax.rsqrt(jnp.mean(y * y, axis=1, keepdims=True) + head_epsilon)
        return (y * jnp.where(part == 2, 1.0, scale)).astype(bf16)

    outs = (o0, o1, o2, o3)
    for slot, out in enumerate(outs):
        lane = pl.multiple_of(((ctx + slot) & 3) * HD, HD)
        out[part] = column(acc[:, pl.ds(lane, HD)])
    z = column(acc[:, 4 * HD : 5 * HD])

    @pl.when(part == 0)
    def _():
        q4[...] = z

    @pl.when(part > 0)
    def _():
        for out in outs:
            out[part + 2] = z


def project(place, own, left, right, far_low, far_high, weight):
    width = own.shape[1]
    model = 4 * width
    half = pl.BlockSpec((HALF, width), lambda j, p: (0, 0))
    quarter = pl.BlockSpec((SUB, width), lambda j, p: (0, 0))
    return pl.pallas_call(
        project_kernel,
        out_shape=(jax.ShapeDtypeStruct((5, HALF, HD), bf16),) * 4
        + (jax.ShapeDtypeStruct((HALF, HD), bf16),),
        grid_spec=pltpu.PrefetchScalarGridSpec(
            num_scalar_prefetch=1,
            grid=(3,),
            in_specs=[half] * 3
            + [quarter] * 2
            + [pl.BlockSpec((1, model, 5 * HD), lambda j, p: (j, 0, 0))],
            out_specs=(pl.BlockSpec((5, HALF, HD), lambda j, p: (0, 0, 0)),) * 4
            + (pl.BlockSpec((HALF, HD), lambda j, p: (0, 0)),),
            scratch_shapes=[
                pltpu.VMEM((HALF, model), bf16),
                pltpu.VMEM((HALF, 5 * HD), f32),
            ],
        ),
        compiler_params=params(),
        cost_estimate=cost(9),
        name="project",
    )(place, own, left, right, far_low, far_high, weight)


def attend_chunk(chunk, query, count_of, ks, vs, acc):
    def add_tile(key_chunk, masked):
        scores = lax.dot_general(
            query, ks[key_chunk], (((1,), (1,)), ((), ())), preferred_element_type=f32
        )
        weights = jnp.exp2(scores * EXP2_SCALE)
        if masked:
            row = lax.broadcasted_iota(jnp.int32, (HALF, HALF), 0)
            col = lax.broadcasted_iota(jnp.int32, (HALF, HALF), 1)
            weights = jnp.where(col <= row, weights, 0.0)
        acc[...] += jnp.dot(weights.astype(bf16), vs[key_chunk], preferred_element_type=f32)

    acc[...] = jnp.zeros_like(acc)

    def body(key_chunk, carry):
        @pl.when(count_of(key_chunk >> 1) > (key_chunk & 1) * HALF)
        def _():
            add_tile(key_chunk, False)

        return carry

    lax.fori_loop(0, chunk, body, 0)
    add_tile(chunk, True)
    total = acc[:, HD:]
    return (acc[:, :HD] / jnp.where(total == 0.0, 1.0, total)).astype(bf16)


def value_rows(value, half, count):
    rows = lax.broadcasted_iota(jnp.int32, (HALF, HD), 0) + half * HALF
    return value, jnp.where(rows < count, 1.0, 0.0).astype(bf16)


def attend_main_kernel(slots, place, *refs):
    inputs, outs, (qs, ks, vs, acc) = refs[:8], refs[8:10], refs[10:]
    ctx = place[0]

    def count_of(block):
        return place[1 + ((ctx - block) & 3)]

    for s in range(4):
        for half in range(2):
            chunk = ((ctx - s) & 3) * 2 + half
            source = inputs[2 * s + half]
            qs[chunk] = source[0]
            ks[chunk] = source[1]
            value, flag = value_rows(source[2], half, place[1 + s])
            vs[chunk, :, :HD] = value
            vs[chunk, :, HD:] = flag

    for s, out in zip(slots, outs):
        count = place[1 + s]

        def body(half, carry):
            chunk = ((ctx - s) & 3) * 2 + half
            filled = count > half * HALF

            @pl.when(filled)
            def _():
                out[half] = attend_chunk(chunk, qs[chunk], count_of, ks, vs, acc)

            @pl.when(jnp.logical_not(filled))
            def _():
                out[half] = jnp.zeros((HALF, HD), bf16)

            return carry

        lax.fori_loop(0, 2, body, 0)


def vmem_specs(count):
    return [pl.BlockSpec(memory_space=pltpu.VMEM)] * count


def attend_main(slots, place, inputs):
    return pl.pallas_call(
        functools.partial(attend_main_kernel, slots),
        out_shape=(jax.ShapeDtypeStruct((2, HALF, HD), bf16),) * 2,
        in_specs=[pl.BlockSpec(memory_space=pltpu.SMEM)] + vmem_specs(8),
        out_specs=tuple(vmem_specs(2)),
        scratch_shapes=[
            pltpu.VMEM((8, HALF, HD), bf16),
            pltpu.VMEM((8, HALF, HD), bf16),
            pltpu.VMEM((8, HALF, 2 * HD), bf16),
            pltpu.VMEM((HALF, 2 * HD), f32),
        ],
        compiler_params=params(),
        cost_estimate=cost(10),
        name="attend_main",
    )(place, *inputs)


def attend_last_kernel(place, q0, q1, *refs):
    inputs, (out, ks, vs, acc) = refs[:8], refs[8:]
    ctx = place[0]

    def count_of(block):
        return place[1 + ((ctx - block) & 3)]

    for s in range(4):

        @pl.when(s <= ctx)
        def _():
            for half in range(2):
                chunk = (ctx - s) * 2 + half
                source = inputs[2 * s + half]
                ks[chunk] = source[3]
                value, flag = value_rows(source[4], half, place[1 + s])
                vs[chunk, :, :HD] = value
                vs[chunk, :, HD:] = flag

    for half, query in enumerate((q0, q1)):
        filled = place[1] > half * HALF

        @pl.when(filled)
        def _():
            out[half] = attend_chunk(ctx * 2 + half, query[...], count_of, ks, vs, acc)

        @pl.when(jnp.logical_not(filled))
        def _():
            out[half] = jnp.zeros((HALF, HD), bf16)


def attend_last(place, queries, inputs):
    return pl.pallas_call(
        attend_last_kernel,
        out_shape=jax.ShapeDtypeStruct((2, HALF, HD), bf16),
        in_specs=[pl.BlockSpec(memory_space=pltpu.SMEM)] + vmem_specs(10),
        out_specs=vmem_specs(1)[0],
        scratch_shapes=[
            pltpu.VMEM((8, HALF, HD), bf16),
            pltpu.VMEM((8, HALF, 2 * HD), bf16),
            pltpu.VMEM((HALF, 2 * HD), f32),
        ],
        compiler_params=params(),
        cost_estimate=cost(4),
        name="attend_last",
    )(place, *queries, *inputs)


def output_kernel(offs_ref, depth_ref, *refs):
    lasts, firsts, thirds, weights = refs[:4], refs[4:9], refs[9:14], refs[14:18]
    out, cbuf, rows = refs[18:]
    step = pl.program_id(0)

    @pl.when(step == 0)
    def _():
        rows[CAP:, :] = jnp.zeros((WINDOW, rows.shape[1]), bf16)
        for half in range(2):
            total = None
            for source in range(4):
                near = source < 3
                for head in range(3):
                    i = 2 * head + half
                    piece = firsts[source][i] if near else firsts[3 + i // 3][i % 3]
                    cbuf[:, head * HD : (head + 1) * HD] = piece
                cbuf[:, 3 * HD : 4 * HD] = thirds[source][half] if near else thirds[3 + half][0]
                cbuf[:, 4 * HD : 5 * HD] = lasts[source][half]
                term = jnp.dot(cbuf[...], weights[source][...], preferred_element_type=f32)
                term = term.astype(bf16).astype(f32)
                total = term if total is None else total + term
            rows[half * HALF : (half + 1) * HALF, :] = total.astype(bf16)

    for sub in range(2):
        offset = offs_ref[step * 2 + sub]
        start = window_start(offset)
        onehot = slot_onehot(depth_ref[sub], offset - start)
        spread = lax.dot_general(
            onehot,
            rows[pl.ds(start, WINDOW), :],
            (((0,), (0,)), ((), ())),
            preferred_element_type=f32,
        )
        out[sub * TOK_BLOCK : (sub + 1) * TOK_BLOCK, :] = spread.astype(bf16)


def output_update(offsets, depth_blocks, groups, weights, length):
    width = weights[0].shape[1]
    steps = length // (2 * TOK_BLOCK)

    def whole(array):
        rank = array.ndim
        return pl.BlockSpec(array.shape, lambda i, o: (0,) * rank)

    return pl.pallas_call(
        output_kernel,
        out_shape=jax.ShapeDtypeStruct((length, width), bf16),
        grid_spec=pltpu.PrefetchScalarGridSpec(
            num_scalar_prefetch=1,
            grid=(steps,),
            in_specs=[pl.BlockSpec((2, 1, TOK_BLOCK), lambda i, o: (i, 0, 0))]
            + [whole(a) for a in groups]
            + [whole(a) for a in weights],
            out_specs=pl.BlockSpec((2 * TOK_BLOCK, width), lambda i, o: (i, 0)),
            scratch_shapes=[
                pltpu.VMEM((HALF, 5 * HD), bf16),
                pltpu.VMEM((ROOM, width), bf16),
            ],
        ),
        compiler_params=params(),
        cost_estimate=cost(14),
        name="output",
    )(offsets, depth_blocks, *groups, *weights)


def shift(value, axis, distance):
    size = lax.axis_size(axis)
    return lax.ppermute(value, axis, [(i, (i + distance) % size) for i in range(size)])


def after(value, *others):
    return lax.optimization_barrier((value, others))[0]


def ring_near(value):
    return [shift(value, "tensor", 1), shift(value, "tensor", -1)]


def ring_far(near):
    middle = near[0].shape[0] // 2
    return [shift(near[0][:middle], "tensor", 1), shift(near[1][middle:], "tensor", -1)]


def per_device(hidden, depth, qkv_weight, out_weight):
    tokens = hidden[0]
    length, width = tokens.shape
    t = lax.axis_index("tensor")
    ctx = lax.axis_index("ctx")
    depth_blocks = depth.reshape(length // TOK_BLOCK, 1, TOK_BLOCK)
    block_counts = jnp.sum((depth_blocks[:, 0] >= RECURSION).astype(jnp.int32), axis=1)
    order = jnp.arange(length // TOK_BLOCK)
    offsets = jnp.sum(
        jnp.where(order[:, None] > order[None, :], block_counts[None, :], 0), axis=1
    ).astype(jnp.int32)
    count = jnp.sum(block_counts).reshape(1)
    counts = jnp.concatenate([count] + [shift(count, "ctx", s) for s in (1, 2, 3)])
    place_ctx = jnp.concatenate([ctx.reshape(1).astype(jnp.int32), counts])
    place_both = jnp.stack([t, ctx]).astype(jnp.int32)
    weight = jnp.transpose(qkv_weight, (1, 0, 2))

    rows = compact_rows(tokens, depth_blocks, offsets)
    (x0, x1), place_ctx = lax.optimization_barrier((rows, place_ctx))

    near0 = ring_near(x0)
    x1 = after(x1, near0)
    far0 = ring_far(near0)
    near1 = ring_near(x1)
    first = project(place_both, x0, *near0, *far0, weight)
    sent0 = [first[0]] + [shift(first[s], "ctx", s) for s in (1, 2, 3)]
    far1 = ring_far(near1)
    second = project(place_both, x1, *near1, *far1, weight)
    second = after(second, sent0)
    sent1 = [second[0]] + [shift(second[s], "ctx", s) for s in (1, 2, 3)]
    arrived = [piece for s in range(4) for piece in (sent0[s], sent1[s])]

    lower = out_weight[: 4 * HD]
    turned = lax.dynamic_slice_in_dim(jnp.concatenate([lower, lower]), ctx * HD, 4 * HD)
    arranged = jnp.concatenate([turned, out_weight[4 * HD :]])
    blocks = [
        lax.dynamic_slice_in_dim(arranged, ((t + distance) & 3) * width, width, axis=1)
        for distance in (0, 1, 3, 2)
    ]
    blocks = after(blocks, far1)
    weights = [blocks[0], shift(blocks[1], "tensor", 1), shift(blocks[2], "tensor", 3)]
    weights.append(shift(after(blocks[3], weights[1:]), "tensor", 2))

    arrived, weights = lax.optimization_barrier((arrived, weights))
    last = attend_last(place_ctx, (first[4], second[4]), arrived)
    lasts = [last] + ring_near(last) + [shift(last, "tensor", 2)]
    to_near, to_far = attend_main((1, 2), place_ctx, after(arrived, last))
    back = [shift(to_near, "ctx", -1), shift(to_far, "ctx", -2)]
    to_right, own = attend_main((3, 0), place_ctx, after(arrived, to_near, to_far, lasts))
    back.append(shift(to_right, "ctx", -3))
    firsts = jnp.concatenate([own, back[0], back[1]])
    near = ring_near(firsts)
    third = after(back[2], near)
    firsts = [firsts] + near + ring_far(near)
    near = ring_near(third)
    thirds = [third] + near + ring_far(near)
    update = output_update(offsets, depth_blocks, lasts + firsts + thirds, weights, length)
    return update[None]


def solution(mesh):
    placed = (P("dp", "ctx", "tensor"), P("dp", "ctx"), P(None, None, "tensor"), P("tensor", None))
    return jax.shard_map(
        per_device, mesh=mesh, in_specs=placed, out_specs=P("dp", "ctx", "tensor"), check_vma=False
    )
```

time: 326 us -> 261 us (0.80)
  the two profiles are of different devices: /device:TPU:1 before, /device:TPU:20 now
where the time goes in v2:
time: 261 us
  waiting for transfers between devices  99.8 us (38%)
  Pallas kernels  94 us (36%)
  starting transfers between devices  47.5 us (18%)
  local copies, waits for them, and re-layouts  12.6 us (5%)
  other arithmetic  6.52 us (2%)
    ppermute x34, waiting for transfers between devices, shift(): lax.ppermute(value, axis, [(i, (i + distance) % size) for i in range(size)])  99.8 us
    ppermute x34, starting transfers between devices, shift(): lax.ppermute(value, axis, [(i, (i + distance) % size) for i in range(size)])  47.5 us
    pallas_call x2, Pallas kernels, attend_main(): pl.pallas_call(functools.partial(attend_main_kernel, slots), out_shape=(j...  28.1 us
    pallas_call x2, Pallas kernels, project(): pl.pallas_call(project_kernel, out_shape=(jax.ShapeDtypeStruct((5, HALF,...  27.7 us
    pallas_call x1, Pallas kernels, output_update(): pl.pallas_call(output_kernel, out_shape=jax.ShapeDtypeStruct((length, wid...  17.8 us
    pallas_call x1, Pallas kernels, compact_rows(): pl.pallas_call(compact_kernel, out_shape=(jax.ShapeDtypeStruct((HALF, wid...  10.4 us
    pallas_call x1, Pallas kernels, attend_last(): pl.pallas_call(attend_last_kernel, out_shape=jax.ShapeDtypeStruct((2, HAL...  9.92 us
    unnamed x64, local copies, waits for them, and re-layouts  6.58 us
  transfers between devices with their start and end apart: 34, of which 17 were waited for; matrix products, arithmetic and copies ran while one was open for 3% of the time, Pallas kernels for 25%

profile of v2, /device:TPU:20, one launch (start us, length us, event | category | flops | bytes accessed | tf_op | source)
XLA Modules:
  0.0 260.7 jit_solution(17702328405981383327)
XLA Ops:
  1.8 2.9 %collective-permute-start.1 = (s32[1]{0:T(128)}, s32[1]{0:T(128)}, u32[]{:S(2)}, u32[]{:S(2)}) collective-permute-start(s32[1]{0:T(128)} %bitcast.3), channel_id=1, source_target_pairs={{0,8},{4,12},{8,0},{12,4},{1,9},{5,13},{9,1},{13,5},{2,10},{6,14},... | collective-permute-start | bytes 20 | tf_op jit(solution)/shard_map/ppermute | solution.py:377
  5.5 10.4 %compact.1 = (bf16[512,640]{1,0:T(8,128)(2,1)}, bf16[512,640]{1,0:T(8,128)(2,1)}) custom-call(s32[16]{0:T(128)} %select_reduce_fusion.offs_ref, s32[16,1,256]{2,1,0:T(1,128)} %bitcast.7, bf16[4096,640]{1,0:T(8,128)(2,1)} %bitcast.11), custom_call_target="tpu_custom_call" | custom-call | flops 8800000000 | tf_op jit(solution)/shard_map/compact/pallas_call | solution.py:81
  15.9 3.0 %concatenate.12.place = s32[5]{0:T(128)} concatenate(s32[1]{0:T(128)} %bitcast.2, s32[1]{0:T(128)} %bitcast.3, s32[1]{0:T(128)} %collective-permute-done, s32[1]{0:T(128)} %collective-permute-done.1, s32[1]{0:T(128)} %collective-permute-done.2), dimensions={0} | concatenate | bytes 40 | tf_op jit(solution)/shard_map/concatenate | solution.py:406
  19.0 4.0 %collective-permute-start.4 = (bf16[512,640]{1,0:T(8,128)(2,1)}, bf16[512,640]{1,0:T(8,128)(2,1)S(1)}, u32[]{:S(2)}, u32[]{:S(2)}) collective-permute-start(bf16[512,640]{1,0:T(8,128)(2,1)} %get-tuple-element.67.x), channel_id=1, source_target_pairs={{0,3},{1,0},{2,1},{3,2},{4,7},{5,4},{6,5},{7,6},{8,11},{9,8},{10,9... | collective-permute-start | bytes 1966088 | tf_op jit(solution)/shard_map/ppermute | solution.py:377
  23.0 13.7 %collective-permute-done.4.b = bf16[512,640]{1,0:T(8,128)(2,1)S(1)} collective-permute-done((bf16[512,640]{1,0:T(8,128)(2,1)}, bf16[512,640]{1,0:T(8,128)(2,1)S(1)}, u32[]{:S(2)}, u32[]{:S(2)}) %collective-permute-start.4) | collective-permute-done | bytes 655392 | tf_op jit(solution)/shard_map/ppermute | solution.py:377
  37.6 2.5 collective-permute-done.3.a
  44.7 2.5 fusion
  47.3 2.4 collective-permute-start.6
  49.8 9.0 %collective-permute-done.8.b = bf16[512,640]{1,0:T(8,128)(2,1)S(1)} collective-permute-done((bf16[512,640]{1,0:T(8,128)(2,1)}, bf16[512,640]{1,0:T(8,128)(2,1)S(1)}, u32[]{:S(2)}, u32[]{:S(2)}) %collective-permute-start.8) | collective-permute-done | bytes 655392 | tf_op jit(solution)/shard_map/ppermute | solution.py:377
  58.8 2.4 collective-permute-start.10
  64.1 5.8 %collective-permute-done.10.d = bf16[256,640]{1,0:T(8,128)(2,1)S(1)} collective-permute-done((bf16[256,640]{1,0:T(8,128)(2,1)S(1)}, bf16[256,640]{1,0:T(8,128)(2,1)S(1)}, u32[]{:S(2)}, u32[]{:S(2)}) %collective-permute-start.10) | collective-permute-done | bytes 327712 | tf_op jit(solution)/shard_map/ppermute | solution.py:377
  69.9 2.3 collective-permute-done.9.c
  72.9 3.2 %collective-permute-start.18 = (bf16[640,640]{1,0:T(8,128)(2,1)S(1)}, bf16[640,640]{1,0:T(8,128)(2,1)S(1)}, u32[]{:S(2)}, u32[]{:S(2)}) collective-permute-start(bf16[640,640]{1,0:T(8,128)(2,1)S(1)} %get-tuple-element.87), channel_id=1, source_target_pairs={{0,3},{1,0},{2,1},{3,2},{4,7},{5,4},{6,5},{7,6},{8,11},{9,8},{10,9... | collective-permute-start | bytes 2457608 | tf_op jit(solution)/shard_map/ppermute | solution.py:377
  77.1 13.8 %project.2 = (bf16[5,512,128]{2,1,0:T(8,128)(2,1)}, bf16[5,512,128]{2,1,0:T(8,128)(2,1)}, bf16[5,512,128]{2,1,0:T(8,128)(2,1)}, bf16[5,512,128]{2,1,0:T(8,128)(2,1)}, bf16[512,128]{1,0:T(8,128)(2,1)}) custom-call(s32[2]{0:T(128)} %pad_add_fusion.place, bf16[512,640]{1,0:T(8,128)(2,1)} %get-tuple-element.67.x, bf16[512,640]{1,0:T(8,128)(2,1)} %copy-done.5, ...), custom_call_target="tpu_custom_call" | custom-call | flops 9900000256 | tf_op jit(solution)/shard_map/project/pallas_call | solution.py:148
  94.9 13.9 %project.3 = (bf16[5,512,128]{2,1,0:T(8,128)(2,1)}, bf16[5,512,128]{2,1,0:T(8,128)(2,1)}, bf16[5,512,128]{2,1,0:T(8,128)(2,1)}, bf16[5,512,128]{2,1,0:T(8,128)(2,1)}, bf16[512,128]{1,0:T(8,128)(2,1)}) custom-call(s32[2]{0:T(128)} %pad_add_fusion.place, bf16[512,640]{1,0:T(8,128)(2,1)} %get-tuple-element.70.x, bf16[512,640]{1,0:T(8,128)(2,1)} %collective-permute-done.7.a, ...), custom_call_target="tpu_custom_call" | custom-call | flops 9900000256 | tf_op jit(solution)/shard_map/project/pallas_call | solution.py:148
  108.8 10.4 %collective-permute-done.12.refs_4_ = bf16[5,512,128]{2,1,0:T(8,128)(2,1)S(1)} collective-permute-done((bf16[5,512,128]{2,1,0:T(8,128)(2,1)}, bf16[5,512,128]{2,1,0:T(8,128)(2,1)S(1)}, u32[]{:S(2)}, u32[]{:S(2)}) %collective-permute-start.12) | collective-permute-done | bytes 655392 | tf_op jit(solution)/shard_map/ppermute | solution.py:377
  123.8 13.4 %collective-permute-done.14.refs_3_ = bf16[5,512,128]{2,1,0:T(8,128)(2,1)S(1)} collective-permute-done((bf16[5,512,128]{2,1,0:T(8,128)(2,1)}, bf16[5,512,128]{2,1,0:T(8,128)(2,1)S(1)}, u32[]{:S(2)}, u32[]{:S(2)}) %collective-permute-start.14) | collective-permute-done | bytes 655392 | tf_op jit(solution)/shard_map/ppermute | solution.py:377
  137.2 14.1 %collective-permute-done.15.refs_5_ = bf16[5,512,128]{2,1,0:T(8,128)(2,1)S(1)} collective-permute-done((bf16[5,512,128]{2,1,0:T(8,128)(2,1)}, bf16[5,512,128]{2,1,0:T(8,128)(2,1)S(1)}, u32[]{:S(2)}, u32[]{:S(2)}) %collective-permute-start.15) | collective-permute-done | bytes 655392 | tf_op jit(solution)/shard_map/ppermute | solution.py:377
  152.9 9.9 %attend_last.1.refs_0_ = bf16[2,512,128]{2,1,0:T(8,128)(2,1)} custom-call(s32[5]{0:T(128)} %concatenate.12.place, bf16[512,128]{1,0:T(8,128)(2,1)} %get-tuple-element.68.q0, bf16[512,128]{1,0:T(8,128)(2,1)} %get-tuple-element.80.q1, bf16[5,512,128]{2,1,0:T(8,128)(2,1)} %get-tuple-element.108.refs_0_, bf16[5,512,128]{2,1,0:T(8,128)(2,1)} %get-tuple-element.109.refs_1_, ...), custom_call_target="tpu_custom_call" | custom-call | flops 4400000000 | tf_op jit(solution)/shard_map/attend_last/pallas_call | solution.py:294
  164.9 9.5 %attend_main.2 = (bf16[2,512,128]{2,1,0:T(8,128)(2,1)}, bf16[2,512,128]{2,1,0:T(8,128)(2,1)}) custom-call(s32[5]{0:T(128)} %concatenate.12.place, bf16[5,512,128]{2,1,0:T(8,128)(2,1)} %get-tuple-element.108.refs_0_, bf16[5,512,128]{2,1,0:T(8,128)(2,1)} %get-tuple-element.109.refs_1_, bf16[5,512,128]{2,1,0:T(8,128)(2,1)} %copy-done.13, ...), custom_call_target="tpu_custom_call" | custom-call | flops 11000000512 | tf_op jit(solution)/shard_map/attend_main/pallas_call | solution.py:245
  174.4 3.5 %collective-permute-start.23 = (bf16[2,512,128]{2,1,0:T(8,128)(2,1)}, bf16[2,512,128]{2,1,0:T(8,128)(2,1)S(1)}, u32[]{:S(2)}, u32[]{:S(2)}) collective-permute-start(bf16[2,512,128]{2,1,0:T(8,128)(2,1)} %get-tuple-element.106), channel_id=1, source_target_pairs={{0,12},{4,0},{8,4},{12,8},{1,13},{5,1},{9,5},{13,9},{2,14},{6,2},{... | collective-permute-start | bytes 786440 | tf_op jit(solution)/shard_map/ppermute | solution.py:377
  177.9 7.5 %collective-permute-start.24 = (bf16[2,512,128]{2,1,0:T(8,128)(2,1)}, bf16[2,512,128]{2,1,0:T(8,128)(2,1)S(1)}, u32[]{:S(2)}, u32[]{:S(2)}) collective-permute-start(bf16[2,512,128]{2,1,0:T(8,128)(2,1)} %get-tuple-element.107), channel_id=1, source_target_pairs={{0,8},{4,12},{8,0},{12,4},{1,9},{5,13},{9,1},{13,5},{2,10},{6,14},... | collective-permute-start | bytes 786440 | tf_op jit(solution)/shard_map/ppermute | solution.py:377
  185.5 18.6 %attend_main.3 = (bf16[2,512,128]{2,1,0:T(8,128)(2,1)}, bf16[2,512,128]{2,1,0:T(8,128)(2,1)}) custom-call(s32[5]{0:T(128)} %concatenate.12.place, bf16[5,512,128]{2,1,0:T(8,128)(2,1)} %get-tuple-element.108.refs_0_, bf16[5,512,128]{2,1,0:T(8,128)(2,1)} %get-tuple-element.109.refs_1_, bf16[5,512,128]{2,1,0:T(8,128)(2,1)} %copy-done.13, ...), custom_call_target="tpu_custom_call" | custom-call | flops 11000000512 | tf_op jit(solution)/shard_map/attend_main/pallas_call | solution.py:245
  205.2 2.9 %collective-permute-start.26 = (bf16[6,512,128]{2,1,0:T(8,128)(2,1)S(1)}, bf16[6,512,128]{2,1,0:T(8,128)(2,1)S(1)}, u32[]{:S(2)}, u32[]{:S(2)}) collective-permute-start(bf16[6,512,128]{2,1,0:T(8,128)(2,1)S(1)} %constant_dynamic-update-slice_fusion.refs_4_), channel_id=1, source_target_pairs={{0,3},{1,0},{2,1},{3,2},{4,7},{5,4},{6,5},{7,6},{8,11},{9,8},{10,9... | collective-permute-start | bytes 2359304 | tf_op jit(solution)/shard_map/ppermute | solution.py:377
  208.2 6.6 %collective-permute-done.29.refs_9_ = bf16[2,512,128]{2,1,0:T(8,128)(2,1)S(1)} collective-permute-done((bf16[2,512,128]{2,1,0:T(8,128)(2,1)}, bf16[2,512,128]{2,1,0:T(8,128)(2,1)S(1)}, u32[]{:S(2)}, u32[]{:S(2)}) %collective-permute-start.29) | collective-permute-done | bytes 262176 | tf_op jit(solution)/shard_map/ppermute | solution.py:377
  214.8 8.1 %collective-permute-done.26.refs_6_ = bf16[6,512,128]{2,1,0:T(8,128)(2,1)S(1)} collective-permute-done((bf16[6,512,128]{2,1,0:T(8,128)(2,1)S(1)}, bf16[6,512,128]{2,1,0:T(8,128)(2,1)S(1)}, u32[]{:S(2)}, u32[]{:S(2)}) %collective-permute-start.26) | collective-permute-done | bytes 786464 | tf_op jit(solution)/shard_map/ppermute | solution.py:377
  222.8 4.0 %collective-permute-done.25.refs_5_ = bf16[6,512,128]{2,1,0:T(8,128)(2,1)S(1)} collective-permute-done((bf16[6,512,128]{2,1,0:T(8,128)(2,1)S(1)}, bf16[6,512,128]{2,1,0:T(8,128)(2,1)S(1)}, u32[]{:S(2)}, u32[]{:S(2)}) %collective-permute-start.25) | collective-permute-done | bytes 786464 | tf_op jit(solution)/shard_map/ppermute | solution.py:377
  228.8 2.0 collective-permute-start.28
  231.0 2.1 collective-permute-done.31.refs_11_
  235.4 2.0 collective-permute-done.28.refs_8_
  238.8 2.6 %collective-permute-done.32.refs_12_ = bf16[1,512,128]{2,1,0:T(8,128)(2,1)S(1)} collective-permute-done((bf16[1,512,128]{2,1,0:T(8,128)(2,1)S(1)}, bf16[1,512,128]{2,1,0:T(8,128)(2,1)S(1)}, u32[]{:S(2)}, u32[]{:S(2)}) %collective-permute-start.32) | collective-permute-done | bytes 131104 | tf_op jit(solution)/shard_map/ppermute | solution.py:377
  242.9 17.8 %output.1 = bf16[4096,640]{1,0:T(8,128)(2,1)} custom-call(s32[16]{0:T(128)} %select_reduce_fusion.offs_ref, s32[16,1,256]{2,1,0:T(1,128)} %bitcast.8, bf16[2,512,128]{2,1,0:T(8,128)(2,1)} %attend_last.1.refs_0_, bf16[2,512,128]{2,1,0:T(8,128)(2,1)} %copy-done.27, bf16[2,512,128]{2,1,0:T(8,128)(2,1)} %copy-done.26, bf16[2,512,128]{2,1,0:T(8,128)(2,1)} %copy-done.25, ...), custom_call_target="tpu_custom_call" | custom-call | flops 15399999488 | tf_op jit(solution)/shard_map/output/pallas_call | solution.py:354
  (128 shorter events, 33.3 us)
Async XLA Ops:
  1.4 14.5 %collective-permute-start.2 = (s32[1]{0:T(128)}, s32[1]{0:T(128)}, u32[]{:S(2)}, u32[]{:S(2)}) collective-permute-start(s32[1]{0:T(128)} %bitcast.3), channel_id=1, source_target_pairs={{0,12},{4,0},{8,4},{12,8},{1,13},{5,1},{9,5},{13,9},{2,14},{6,2},{... | collective-permute-start | bytes 20 | tf_op jit(solution)/shard_map/ppermute | solution.py:377
  1.8 14.1 %collective-permute-start.1 = (s32[1]{0:T(128)}, s32[1]{0:T(128)}, u32[]{:S(2)}, u32[]{:S(2)}) collective-permute-start(s32[1]{0:T(128)} %bitcast.3), channel_id=1, source_target_pairs={{0,8},{4,12},{8,0},{12,4},{1,9},{5,13},{9,1},{13,5},{2,10},{6,14},... | collective-permute-start | bytes 20 | tf_op jit(solution)/shard_map/ppermute | solution.py:377
  4.7 11.2 %collective-permute-start = (s32[1]{0:T(128)}, s32[1]{0:T(128)}, u32[]{:S(2)}, u32[]{:S(2)}) collective-permute-start(s32[1]{0:T(128)} %bitcast.3), channel_id=1, source_target_pairs={{0,4},{4,8},{8,12},{12,0},{1,5},{5,9},{9,13},{13,1},{2,6},{6,10},{... | collective-permute-start | bytes 20 | tf_op jit(solution)/shard_map/ppermute | solution.py:377
  19.0 17.8 %collective-permute-start.4 = (bf16[512,640]{1,0:T(8,128)(2,1)}, bf16[512,640]{1,0:T(8,128)(2,1)S(1)}, u32[]{:S(2)}, u32[]{:S(2)}) collective-permute-start(bf16[512,640]{1,0:T(8,128)(2,1)} %get-tuple-element.67.x), channel_id=1, source_target_pairs={{0,3},{1,0},{2,1},{3,2},{4,7},{5,4},{6,5},{7,6},{8,11},{9,8},{10,9... | collective-permute-start | bytes 1966088 | tf_op jit(solution)/shard_map/ppermute | solution.py:377
  23.0 17.1 %collective-permute-start.3 = (bf16[512,640]{1,0:T(8,128)(2,1)}, bf16[512,640]{1,0:T(8,128)(2,1)S(1)}, u32[]{:S(2)}, u32[]{:S(2)}) collective-permute-start(bf16[512,640]{1,0:T(8,128)(2,1)} %get-tuple-element.67.x), channel_id=1, source_target_pairs={{0,1},{1,2},{2,3},{3,0},{4,5},{5,6},{6,7},{7,4},{8,9},{9,10},{10,1... | collective-permute-start | bytes 1966088 | tf_op jit(solution)/shard_map/ppermute | solution.py:377
  40.9 17.9 %collective-permute-start.8 = (bf16[512,640]{1,0:T(8,128)(2,1)}, bf16[512,640]{1,0:T(8,128)(2,1)S(1)}, u32[]{:S(2)}, u32[]{:S(2)}) collective-permute-start(bf16[512,640]{1,0:T(8,128)(2,1)} %get-tuple-element.70.x), channel_id=1, source_target_pairs={{0,3},{1,0},{2,1},{3,2},{4,7},{5,4},{6,5},{7,6},{8,11},{9,8},{10,9... | collective-permute-start | bytes 1966088 | tf_op jit(solution)/shard_map/ppermute | solution.py:377
  42.0 19.2 %collective-permute-start.7 = (bf16[512,640]{1,0:T(8,128)(2,1)}, bf16[512,640]{1,0:T(8,128)(2,1)}, u32[]{:S(2)}, u32[]{:S(2)}) collective-permute-start(bf16[512,640]{1,0:T(8,128)(2,1)} %get-tuple-element.70.x), channel_id=1, source_target_pairs={{0,1},{1,2},{2,3},{3,0},{4,5},{5,6},{6,7},{7,4},{8,9},{9,10},{10,1... | collective-permute-start | bytes 1966088 | tf_op jit(solution)/shard_map/ppermute | solution.py:377
  47.3 28.9 %collective-permute-start.6 = (bf16[256,640]{1,0:T(8,128)(2,1)S(1)}, bf16[256,640]{1,0:T(8,128)(2,1)S(1)}, u32[]{:S(2)}, u32[]{:S(2)}) collective-permute-start(bf16[256,640]{1,0:T(8,128)(2,1)S(1)} %slice.41), channel_id=1, source_target_pairs={{0,3},{1,0},{2,1},{3,2},{4,7},{5,4},{6,5},{7,6},{8,11},{9,8},{10,9... | collective-permute-start | bytes 983048 | tf_op jit(solution)/shard_map/ppermute | solution.py:377
  49.7 26.4 %collective-permute-start.5 = (bf16[256,640]{1,0:T(8,128)(2,1)S(1)}, bf16[256,640]{1,0:T(8,128)(2,1)S(1)}, u32[]{:S(2)}, u32[]{:S(2)}) collective-permute-start(bf16[256,640]{1,0:T(8,128)(2,1)S(1)} %slice.40), channel_id=1, source_target_pairs={{0,1},{1,2},{2,3},{3,0},{4,5},{5,6},{6,7},{7,4},{8,9},{9,10},{10,1... | collective-permute-start | bytes 983048 | tf_op jit(solution)/shard_map/ppermute | solution.py:377
  58.8 11.0 %collective-permute-start.10 = (bf16[256,640]{1,0:T(8,128)(2,1)S(1)}, bf16[256,640]{1,0:T(8,128)(2,1)S(1)}, u32[]{:S(2)}, u32[]{:S(2)}) collective-permute-start(bf16[256,640]{1,0:T(8,128)(2,1)S(1)} %slice.43), channel_id=1, source_target_pairs={{0,3},{1,0},{2,1},{3,2},{4,7},{5,4},{6,5},{7,6},{8,11},{9,8},{10,9... | collective-permute-start | bytes 983048 | tf_op jit(solution)/shard_map/ppermute | solution.py:377
  62.2 10.0 %collective-permute-start.9 = (bf16[256,640]{1,0:T(8,128)(2,1)S(1)}, bf16[256,640]{1,0:T(8,128)(2,1)S(1)}, u32[]{:S(2)}, u32[]{:S(2)}) collective-permute-start(bf16[256,640]{1,0:T(8,128)(2,1)S(1)} %slice.42), channel_id=1, source_target_pairs={{0,1},{1,2},{2,3},{3,0},{4,5},{5,6},{6,7},{7,4},{8,9},{9,10},{10,1... | collective-permute-start | bytes 983048 | tf_op jit(solution)/shard_map/ppermute | solution.py:377
  72.9 21.9 %collective-permute-start.17 = (bf16[640,640]{1,0:T(8,128)(2,1)S(1)}, bf16[640,640]{1,0:T(8,128)(2,1)S(1)}, u32[]{:S(2)}, u32[]{:S(2)}) collective-permute-start(bf16[640,640]{1,0:T(8,128)(2,1)S(1)} %get-tuple-element.86), channel_id=1, source_target_pairs={{0,1},{1,2},{2,3},{3,0},{4,5},{5,6},{6,7},{7,4},{8,9},{9,10},{10,1... | collective-permute-start | bytes 2457608 | tf_op jit(solution)/shard_map/ppermute | solution.py:377
  72.9 21.9 %collective-permute-start.18 = (bf16[640,640]{1,0:T(8,128)(2,1)S(1)}, bf16[640,640]{1,0:T(8,128)(2,1)S(1)}, u32[]{:S(2)}, u32[]{:S(2)}) collective-permute-start(bf16[640,640]{1,0:T(8,128)(2,1)S(1)} %get-tuple-element.87), channel_id=1, source_target_pairs={{0,3},{1,0},{2,1},{3,2},{4,7},{5,4},{6,5},{7,6},{8,11},{9,8},{10,9... | collective-permute-start | bytes 2457608 | tf_op jit(solution)/shard_map/ppermute | solution.py:377
  90.9 17.9 %collective-permute-start.11 = (bf16[5,512,128]{2,1,0:T(8,128)(2,1)}, bf16[5,512,128]{2,1,0:T(8,128)(2,1)S(1)}, u32[]{:S(2)}, u32[]{:S(2)}) collective-permute-start(bf16[5,512,128]{2,1,0:T(8,128)(2,1)} %get-tuple-element.77), channel_id=1, source_target_pairs={{0,4},{4,8},{8,12},{12,0},{1,5},{5,9},{9,13},{13,1},{2,6},{6,10},{... | collective-permute-start | bytes 1966088 | tf_op jit(solution)/shard_map/ppermute | solution.py:377
  92.4 26.8 %collective-permute-start.12 = (bf16[5,512,128]{2,1,0:T(8,128)(2,1)}, bf16[5,512,128]{2,1,0:T(8,128)(2,1)S(1)}, u32[]{:S(2)}, u32[]{:S(2)}) collective-permute-start(bf16[5,512,128]{2,1,0:T(8,128)(2,1)} %get-tuple-element.78), channel_id=1, source_target_pairs={{0,8},{4,12},{8,0},{12,4},{1,9},{5,13},{9,1},{13,5},{2,10},{6,14},... | collective-permute-start | bytes 1966088 | tf_op jit(solution)/shard_map/ppermute | solution.py:377
  94.0 26.4 %collective-permute-start.13 = (bf16[5,512,128]{2,1,0:T(8,128)(2,1)}, bf16[5,512,128]{2,1,0:T(8,128)(2,1)S(1)}, u32[]{:S(2)}, u32[]{:S(2)}) collective-permute-start(bf16[5,512,128]{2,1,0:T(8,128)(2,1)} %get-tuple-element.79), channel_id=1, source_target_pairs={{0,12},{4,0},{8,4},{12,8},{1,13},{5,1},{9,5},{13,9},{2,14},{6,2},{... | collective-permute-start | bytes 1966088 | tf_op jit(solution)/shard_map/ppermute | solution.py:377
  94.8 57.1 %collective-permute-start.19 = (bf16[640,640]{1,0:T(8,128)(2,1)S(1)}, bf16[640,640]{1,0:T(8,128)(2,1)S(1)}, u32[]{:S(2)}, u32[]{:S(2)}) collective-permute-start(bf16[640,640]{1,0:T(8,128)(2,1)S(1)} %get-tuple-element.89), channel_id=1, source_target_pairs={{0,2},{1,3},{2,0},{3,1},{4,6},{5,7},{6,4},{7,5},{8,10},{9,11},{10,... | collective-permute-start | bytes 2457608 | tf_op jit(solution)/shard_map/ppermute | solution.py:377
  120.4 16.8 %collective-permute-start.14 = (bf16[5,512,128]{2,1,0:T(8,128)(2,1)}, bf16[5,512,128]{2,1,0:T(8,128)(2,1)S(1)}, u32[]{:S(2)}, u32[]{:S(2)}) collective-permute-start(bf16[5,512,128]{2,1,0:T(8,128)(2,1)} %get-tuple-element.82), channel_id=1, source_target_pairs={{0,4},{4,8},{8,12},{12,0},{1,5},{5,9},{9,13},{13,1},{2,6},{6,10},{... | collective-permute-start | bytes 1966088 | tf_op jit(solution)/shard_map/ppermute | solution.py:377
  121.8 29.5 %collective-permute-start.15 = (bf16[5,512,128]{2,1,0:T(8,128)(2,1)}, bf16[5,512,128]{2,1,0:T(8,128)(2,1)S(1)}, u32[]{:S(2)}, u32[]{:S(2)}) collective-permute-start(bf16[5,512,128]{2,1,0:T(8,128)(2,1)} %get-tuple-element.83), channel_id=1, source_target_pairs={{0,8},{4,12},{8,0},{12,4},{1,9},{5,13},{9,1},{13,5},{2,10},{6,14},... | collective-permute-start | bytes 1966088 | tf_op jit(solution)/shard_map/ppermute | solution.py:377
  122.9 29.1 %collective-permute-start.16 = (bf16[5,512,128]{2,1,0:T(8,128)(2,1)}, bf16[5,512,128]{2,1,0:T(8,128)(2,1)S(1)}, u32[]{:S(2)}, u32[]{:S(2)}) collective-permute-start(bf16[5,512,128]{2,1,0:T(8,128)(2,1)} %get-tuple-element.84), channel_id=1, source_target_pairs={{0,12},{4,0},{8,4},{12,8},{1,13},{5,1},{9,5},{13,9},{2,14},{6,2},{... | collective-permute-start | bytes 1966088 | tf_op jit(solution)/shard_map/ppermute | solution.py:377
  162.8 22.6 %collective-permute-start.22 = (bf16[2,512,128]{2,1,0:T(8,128)(2,1)}, bf16[2,512,128]{2,1,0:T(8,128)(2,1)S(1)}, u32[]{:S(2)}, u32[]{:S(2)}) collective-permute-start(bf16[2,512,128]{2,1,0:T(8,128)(2,1)} %attend_last.1.refs_0_), channel_id=1, source_target_pairs={{0,2},{1,3},{2,0},{3,1},{4,6},{5,7},{6,4},{7,5},{8,10},{9,11},{10,... | collective-permute-start | bytes 786440 | tf_op jit(solution)/shard_map/ppermute | solution.py:377
  162.8 22.6 %collective-permute-start.21 = (bf16[2,512,128]{2,1,0:T(8,128)(2,1)}, bf16[2,512,128]{2,1,0:T(8,128)(2,1)S(1)}, u32[]{:S(2)}, u32[]{:S(2)}) collective-permute-start(bf16[2,512,128]{2,1,0:T(8,128)(2,1)} %attend_last.1.refs_0_), channel_id=1, source_target_pairs={{0,3},{1,0},{2,1},{3,2},{4,7},{5,4},{6,5},{7,6},{8,11},{9,8},{10,9... | collective-permute-start | bytes 786440 | tf_op jit(solution)/shard_map/ppermute | solution.py:377
  164.5 20.9 %collective-permute-start.20 = (bf16[2,512,128]{2,1,0:T(8,128)(2,1)}, bf16[2,512,128]{2,1,0:T(8,128)(2,1)S(1)}, u32[]{:S(2)}, u32[]{:S(2)}) collective-permute-start(bf16[2,512,128]{2,1,0:T(8,128)(2,1)} %attend_last.1.refs_0_), channel_id=1, source_target_pairs={{0,1},{1,2},{2,3},{3,0},{4,5},{5,6},{6,7},{7,4},{8,9},{9,10},{10,1... | collective-permute-start | bytes 786440 | tf_op jit(solution)/shard_map/ppermute | solution.py:377
  174.4 30.7 %collective-permute-start.23 = (bf16[2,512,128]{2,1,0:T(8,128)(2,1)}, bf16[2,512,128]{2,1,0:T(8,128)(2,1)S(1)}, u32[]{:S(2)}, u32[]{:S(2)}) collective-permute-start(bf16[2,512,128]{2,1,0:T(8,128)(2,1)} %get-tuple-element.106), channel_id=1, source_target_pairs={{0,12},{4,0},{8,4},{12,8},{1,13},{5,1},{9,5},{13,9},{2,14},{6,2},{... | collective-permute-start | bytes 786440 | tf_op jit(solution)/shard_map/ppermute | solution.py:377
  177.9 27.3 %collective-permute-start.24 = (bf16[2,512,128]{2,1,0:T(8,128)(2,1)}, bf16[2,512,128]{2,1,0:T(8,128)(2,1)S(1)}, u32[]{:S(2)}, u32[]{:S(2)}) collective-permute-start(bf16[2,512,128]{2,1,0:T(8,128)(2,1)} %get-tuple-element.107), channel_id=1, source_target_pairs={{0,8},{4,12},{8,0},{12,4},{1,9},{5,13},{9,1},{13,5},{2,10},{6,14},... | collective-permute-start | bytes 786440 | tf_op jit(solution)/shard_map/ppermute | solution.py:377
  205.2 17.6 %collective-permute-start.26 = (bf16[6,512,128]{2,1,0:T(8,128)(2,1)S(1)}, bf16[6,512,128]{2,1,0:T(8,128)(2,1)S(1)}, u32[]{:S(2)}, u32[]{:S(2)}) collective-permute-start(bf16[6,512,128]{2,1,0:T(8,128)(2,1)S(1)} %constant_dynamic-update-slice_fusion.refs_4_), channel_id=1, source_target_pairs={{0,3},{1,0},{2,1},{3,2},{4,7},{5,4},{6,5},{7,6},{8,11},{9,8},{10,9... | collective-permute-start | bytes 2359304 | tf_op jit(solution)/shard_map/ppermute | solution.py:377
  208.2 18.6 %collective-permute-start.25 = (bf16[6,512,128]{2,1,0:T(8,128)(2,1)S(1)}, bf16[6,512,128]{2,1,0:T(8,128)(2,1)S(1)}, u32[]{:S(2)}, u32[]{:S(2)}) collective-permute-start(bf16[6,512,128]{2,1,0:T(8,128)(2,1)S(1)} %constant_dynamic-update-slice_fusion.refs_4_), channel_id=1, source_target_pairs={{0,1},{1,2},{2,3},{3,0},{4,5},{5,6},{6,7},{7,4},{8,9},{9,10},{10,1... | collective-permute-start | bytes 2359304 | tf_op jit(solution)/shard_map/ppermute | solution.py:377
  208.2 6.6 %collective-permute-start.29 = (bf16[2,512,128]{2,1,0:T(8,128)(2,1)}, bf16[2,512,128]{2,1,0:T(8,128)(2,1)S(1)}, u32[]{:S(2)}, u32[]{:S(2)}) collective-permute-start(bf16[2,512,128]{2,1,0:T(8,128)(2,1)} %get-tuple-element.117), channel_id=1, source_target_pairs={{0,4},{4,8},{8,12},{12,0},{1,5},{5,9},{9,13},{13,1},{2,6},{6,10},{... | collective-permute-start | bytes 786440 | tf_op jit(solution)/shard_map/ppermute | solution.py:377
  226.8 6.4 %collective-permute-start.31 = (bf16[2,512,128]{2,1,0:T(8,128)(2,1)S(1)}, bf16[2,512,128]{2,1,0:T(8,128)(2,1)S(1)}, u32[]{:S(2)}, u32[]{:S(2)}) collective-permute-start(bf16[2,512,128]{2,1,0:T(8,128)(2,1)S(1)} %collective-permute-done.29.refs_9_), channel_id=1, source_target_pairs={{0,3},{1,0},{2,1},{3,2},{4,7},{5,4},{6,5},{7,6},{8,11},{9,8},{10,9... | collective-permute-start | bytes 786440 | tf_op jit(solution)/shard_map/ppermute | solution.py:377
  227.5 7.7 %collective-permute-start.30 = (bf16[2,512,128]{2,1,0:T(8,128)(2,1)S(1)}, bf16[2,512,128]{2,1,0:T(8,128)(2,1)S(1)}, u32[]{:S(2)}, u32[]{:S(2)}) collective-permute-start(bf16[2,512,128]{2,1,0:T(8,128)(2,1)S(1)} %collective-permute-done.29.refs_9_), channel_id=1, source_target_pairs={{0,1},{1,2},{2,3},{3,0},{4,5},{5,6},{6,7},{7,4},{8,9},{9,10},{10,1... | collective-permute-start | bytes 786440 | tf_op jit(solution)/shard_map/ppermute | solution.py:377
  228.8 8.5 %collective-permute-start.28 = (bf16[3,512,128]{2,1,0:T(8,128)(2,1)S(1)}, bf16[3,512,128]{2,1,0:T(8,128)(2,1)S(1)}, u32[]{:S(2)}, u32[]{:S(2)}) collective-permute-start(bf16[3,512,128]{2,1,0:T(8,128)(2,1)S(1)} %slice.45), channel_id=1, source_target_pairs={{0,3},{1,0},{2,1},{3,2},{4,7},{5,4},{6,5},{7,6},{8,11},{9,8},{10,9... | collective-permute-start | bytes 1179656 | tf_op jit(solution)/shard_map/ppermute | solution.py:377
  230.9 10.6 %collective-permute-start.27 = (bf16[3,512,128]{2,1,0:T(8,128)(2,1)S(1)}, bf16[3,512,128]{2,1,0:T(8,128)(2,1)S(1)}, u32[]{:S(2)}, u32[]{:S(2)}) collective-permute-start(bf16[3,512,128]{2,1,0:T(8,128)(2,1)S(1)} %slice.44), channel_id=1, source_target_pairs={{0,1},{1,2},{2,3},{3,0},{4,5},{5,6},{6,7},{7,4},{8,9},{9,10},{10,1... | collective-permute-start | bytes 1179656 | tf_op jit(solution)/shard_map/ppermute | solution.py:377
  (35 other events, 405.2 us)

commit v3 on v2

v3 whole, which is shorter than its diff:
```python
import functools
import math

import jax
import jax.numpy as jnp
from jax import lax
from jax.experimental import pallas as pl
from jax.experimental.pallas import tpu as pltpu
from jax.sharding import PartitionSpec as P

HD = 128
RECURSION = 3
CAP = 1024
HALF = CAP // 2
SUB = CAP // 4
TOK_BLOCK = 256
WINDOW = TOK_BLOCK + 16
SMALL = 128
STEP_BLOCKS = 4
SHARES = 4
ROOM = CAP + WINDOW

score_scale = 0.25
norm_epsilon = 1e-05
head_epsilon = 1e-06
EXP2_SCALE = score_scale / math.log(2.0)
MEBI = 1024 * 1024

bf16 = jnp.bfloat16
f32 = jnp.float32


def cost(micros):
    return pl.CostEstimate(flops=int(micros * 1.1e9), bytes_accessed=0, transcendentals=0)


def params(mebibytes):
    return pltpu.CompilerParams(vmem_limit_bytes=mebibytes * MEBI)


def fill_slots(depth_ref, slots):
    active = depth_ref[...] >= RECURSION
    flags = jnp.where(active, 1.0, 0.0).astype(bf16)
    before = lax.broadcasted_iota(jnp.int32, (TOK_BLOCK, TOK_BLOCK), 0)
    after_it = lax.broadcasted_iota(jnp.int32, (TOK_BLOCK, TOK_BLOCK), 1)
    earlier = jnp.where(before < after_it, 1.0, 0.0).astype(bf16)
    rank = jnp.dot(flags, earlier, preferred_element_type=f32).astype(jnp.int32)
    slots[...] = jnp.where(active, rank, -2 * CAP)


def window_onehot(slots, block, shift_by, window):
    rows = lax.broadcasted_iota(jnp.int32, (window, TOK_BLOCK), 0)
    return jnp.where(rows == slots[pl.ds(block, 1), :] + shift_by, 1.0, 0.0).astype(bf16)


def by_window(offs_ref, block, run):
    low, high = offs_ref[block], offs_ref[block + 1]
    start = pl.multiple_of((low >> 4) << 4, 16)

    @pl.when(high - start <= SMALL)
    def _():
        run(start, low - start, SMALL)

    @pl.when(high - start > SMALL)
    def _():
        run(start, low - start, WINDOW)


def compact_kernel(offs_ref, depth_ref, tok_ref, o0, o1, buf, slots):
    step = pl.program_id(0)

    @pl.when(step == 0)
    def _():
        buf[...] = jnp.zeros_like(buf)
        fill_slots(depth_ref, slots)

    def body(sub, carry):
        block = step * STEP_BLOCKS + sub
        at = pl.multiple_of(sub * TOK_BLOCK, TOK_BLOCK)

        def run(start, shift_by, window):
            picked = jnp.dot(
                window_onehot(slots, block, shift_by, window),
                tok_ref[pl.ds(at, TOK_BLOCK), :],
                preferred_element_type=f32,
            ).astype(bf16)
            buf[pl.ds(start, window), :] = buf[pl.ds(start, window), :] + picked

        by_window(offs_ref, block, run)
        return carry

    lax.fori_loop(0, STEP_BLOCKS, body, 0)

    @pl.when(step == pl.num_programs(0) - 1)
    def _():
        for i, o in enumerate((o0, o1)):
            o[...] = buf[i * HALF : (i + 1) * HALF, :]


def compact_rows(tokens, depth_blocks, offsets):
    length, width = tokens.shape
    blocks = length // TOK_BLOCK
    rows = STEP_BLOCKS * TOK_BLOCK
    return pl.pallas_call(
        compact_kernel,
        out_shape=(jax.ShapeDtypeStruct((HALF, width), bf16),) * 2,
        grid_spec=pltpu.PrefetchScalarGridSpec(
            num_scalar_prefetch=1,
            grid=(length // rows,),
            in_specs=[
                pl.BlockSpec((blocks, TOK_BLOCK), lambda i, o: (0, 0)),
                pl.BlockSpec((rows, width), lambda i, o: (i, 0)),
            ],
            out_specs=(pl.BlockSpec((HALF, width), lambda i, o: (0, 0)),) * 2,
            scratch_shapes=[
                pltpu.VMEM((ROOM, width), bf16),
                pltpu.VMEM((blocks, TOK_BLOCK), jnp.int32),
            ],
        ),
        compiler_params=params(12),
        cost_estimate=cost(8),
        name="compact",
    )(offsets, depth_blocks, tokens)


def project_kernel(place, x, a, b, c, d, w_ref, o0, o1, o2, o3, q4, xs, acc):
    t = place[0]
    ctx = place[1]
    width = x.shape[1]
    for sub, far in enumerate((c, d)):
        low = sub * SUB
        pieces = [p[low : low + SUB, :] for p in (x, a, b)] + [far[...]]
        squares = jnp.zeros((SUB, 1), f32)
        for piece in pieces:
            wide = piece.astype(f32)
            squares = squares + jnp.sum(wide * wide, axis=1, keepdims=True)
        factor = lax.rsqrt(squares * (1.0 / (4 * width)) + norm_epsilon)
        for distance, piece in zip((0, 3, 1, 2), pieces):
            lane = pl.multiple_of(((t + distance) & 3) * width, 128)
            normed = (piece.astype(f32) * factor).astype(bf16)
            xs[low : low + SUB, pl.ds(lane, width)] = normed

    outs = (o0, o1, o2, o3)

    def body(part, carry):
        acc[...] = jnp.dot(xs[...], w_ref[part], preferred_element_type=f32)

        def column(y):
            scale = lax.rsqrt(jnp.mean(y * y, axis=1, keepdims=True) + head_epsilon)
            return (y * jnp.where(part == 2, 1.0, scale)).astype(bf16)

        for slot, out in enumerate(outs):
            lane = pl.multiple_of(((ctx + slot) & 3) * HD, HD)
            out[part] = column(acc[:, pl.ds(lane, HD)])
        z = column(acc[:, 4 * HD : 5 * HD])

        @pl.when(part == 0)
        def _():
            q4[...] = z

        @pl.when(part > 0)
        def _():
            for out in outs:
                out[part + 2] = z

        return carry

    lax.fori_loop(0, 3, body, 0)


def project(place, own, left, right, far_low, far_high, weight, micros):
    width = own.shape[1]
    return pl.pallas_call(
        project_kernel,
        out_shape=(jax.ShapeDtypeStruct((5, HALF, HD), bf16),) * 4
        + (jax.ShapeDtypeStruct((HALF, HD), bf16),),
        in_specs=[pl.BlockSpec(memory_space=pltpu.SMEM)] + vmem_specs(6),
        out_specs=tuple(vmem_specs(5)),
        scratch_shapes=[
            pltpu.VMEM((HALF, 4 * width), bf16),
            pltpu.VMEM((HALF, 5 * HD), f32),
        ],
        compiler_params=params(16),
        cost_estimate=cost(micros),
        name="project",
    )(place, own, left, right, far_low, far_high, weight)


def attend_block(block, count, query, count_of, ks, vs, acc):
    def add_tiles(chunk, base=None):
        scores = [
            jnp.dot(query[at : at + HALF, :], ks[chunk], preferred_element_type=f32)
            for at in (0, HALF)
        ]
        for at, score in zip((0, HALF), scores):
            weights = jnp.exp2(score * EXP2_SCALE)
            if base is not None:
                row = lax.broadcasted_iota(jnp.int32, (HALF, HALF), 0) + (at - base)
                col = lax.broadcasted_iota(jnp.int32, (HALF, HALF), 1)
                weights = jnp.where(col <= row, weights, 0.0)
            acc[at : at + HALF, :] += jnp.dot(
                weights.astype(bf16), vs[chunk], preferred_element_type=f32
            )

    acc[...] = jnp.zeros_like(acc)

    @pl.when(count > 0)
    def _():
        def earlier(chunk, carry):
            @pl.when(count_of(chunk >> 1) > (chunk & 1) * HALF)
            def _():
                add_tiles(chunk)

            return carry

        def same(half, carry):
            @pl.when(count > half * HALF)
            def _():
                add_tiles(2 * block + half, half * HALF)

            return carry

        lax.fori_loop(0, 2 * block, earlier, 0)
        lax.fori_loop(0, 2, same, 0)


def context_of(acc, low):
    total = acc[low : low + HALF, HD:]
    return (acc[low : low + HALF, :HD] / jnp.where(total == 0.0, 1.0, total)).astype(bf16)


def place_keys(chunk, half, count, key, value, ks, vs):
    @pl.when(count > half * HALF)
    def _():
        ks[chunk] = key.T
        rows = lax.broadcasted_iota(jnp.int32, (HALF, HD), 0) + half * HALF
        vs[chunk, :, :HD] = value
        vs[chunk, :, HD:] = jnp.where(rows < count, 1.0, 0.0).astype(bf16)


def attend_main_kernel(first_slot, place, *refs):
    inputs, outs, (qs, ks, vs, cs, acc) = refs[:8], refs[8:10], refs[10:]
    ctx = place[0]

    def count_of(block):
        return place[1 + ((ctx - block) & 3)]

    for s in range(4):
        block = (ctx - s) & 3
        for half in range(2):
            source = inputs[2 * s + half]
            qs[s, half * HALF : (half + 1) * HALF] = source[0]
            place_keys(2 * block + half, half, place[1 + s], source[1], source[2], ks, vs)

    def body(i, carry):
        s = (first_slot + i) & 3
        attend_block((ctx - s) & 3, place[1 + s], qs.at[s], count_of, ks, vs, acc)
        for half in range(2):
            cs[i, half] = context_of(acc, half * HALF)
        return carry

    lax.fori_loop(0, 2, body, 0)
    for i, out in enumerate(outs):
        out[...] = cs[i]


def vmem_specs(count):
    return [pl.BlockSpec(memory_space=pltpu.VMEM)] * count


def attend_main(first_slot, place, inputs):
    return pl.pallas_call(
        functools.partial(attend_main_kernel, first_slot),
        out_shape=(jax.ShapeDtypeStruct((2, HALF, HD), bf16),) * 2,
        in_specs=[pl.BlockSpec(memory_space=pltpu.SMEM)] + vmem_specs(8),
        out_specs=tuple(vmem_specs(2)),
        scratch_shapes=[
            pltpu.VMEM((4, CAP, HD), bf16),
            pltpu.VMEM((8, HD, HALF), bf16),
            pltpu.VMEM((8, HALF, 2 * HD), bf16),
            pltpu.VMEM((2, 2, HALF, HD), bf16),
            pltpu.VMEM((CAP, 2 * HD), f32),
        ],
        compiler_params=params(16),
        cost_estimate=cost(10),
        name="attend_main",
    )(place, *inputs)


def attend_last_kernel(place, q0, q1, *refs):
    inputs, (out, qs, ks, vs, acc) = refs[:8], refs[8:]
    ctx = place[0]

    def count_of(block):
        return place[1 + ((ctx - block) & 3)]

    for s in range(4):

        @pl.when(s <= ctx)
        def _():
            for half in range(2):
                source = inputs[2 * s + half]
                chunk = (ctx - s) * 2 + half
                place_keys(chunk, half, place[1 + s], source[3], source[4], ks, vs)

    qs[:HALF, :] = q0[...]
    qs[HALF:, :] = q1[...]
    attend_block(ctx, place[1], qs, count_of, ks, vs, acc)
    for half in range(2):
        out[half] = context_of(acc, half * HALF)


def attend_last(place, queries, inputs):
    return pl.pallas_call(
        attend_last_kernel,
        out_shape=jax.ShapeDtypeStruct((2, HALF, HD), bf16),
        in_specs=[pl.BlockSpec(memory_space=pltpu.SMEM)] + vmem_specs(10),
        out_specs=vmem_specs(1)[0],
        scratch_shapes=[
            pltpu.VMEM((CAP, HD), bf16),
            pltpu.VMEM((8, HD, HALF), bf16),
            pltpu.VMEM((8, HALF, 2 * HD), bf16),
            pltpu.VMEM((CAP, 2 * HD), f32),
        ],
        compiler_params=params(16),
        cost_estimate=cost(4),
        name="attend_last",
    )(place, *queries, *inputs)


def group_term(pieces, weight, cbuf):
    for i, piece in enumerate(pieces):
        cbuf[:, i * HD : (i + 1) * HD] = piece
    term = jnp.dot(cbuf[...], weight, preferred_element_type=f32)
    return term.astype(bf16).astype(f32)


def whole_block(gathered, which, dp):
    places = []
    for share in range(SHARES):
        other = (dp & (SHARES - 1)) ^ share
        places.append((other >> 1) + 2 * (other & 1))
    parts = [gathered[place, which, slot] for slot in range(5) for place in places]
    return jnp.concatenate(parts, axis=0)


def near_terms_kernel(place, *refs):
    lasts, firsts, thirds, (own, gathered), (out, cbuf) = (
        refs[:3],
        refs[3:6],
        refs[6:9],
        refs[9:11],
        refs[11:],
    )
    for source, (last, first, third) in enumerate(zip(lasts, firsts, thirds)):
        if source == 0:
            starts = [pl.multiple_of(((place[0] + slot) & 3) * HD, HD) for slot in range(4)]
            parts = [own[pl.ds(start, HD), :] for start in starts]
            weight = jnp.concatenate(parts + [own[4 * HD :, :]], axis=0)
        else:
            weight = whole_block(gathered, source - 1, place[5])
        for half in range(2):
            at = slice(half * HALF, (half + 1) * HALF)
            pieces = [first[2 * head + half] for head in range(3)] + [third[half], last[half]]
            term = group_term(pieces, weight, cbuf)
            out[at, :] = term if source == 0 else out[at, :] + term


def near_terms(place, lasts, firsts, thirds, own_block, gathered):
    return pl.pallas_call(
        near_terms_kernel,
        out_shape=jax.ShapeDtypeStruct((CAP, own_block.shape[1]), f32),
        in_specs=[pl.BlockSpec(memory_space=pltpu.SMEM)] + vmem_specs(11),
        out_specs=vmem_specs(1)[0],
        scratch_shapes=[pltpu.VMEM((HALF, 5 * HD), bf16)],
        compiler_params=params(12),
        cost_estimate=cost(5),
        name="near_terms",
    )(place, *lasts, *firsts, *thirds, own_block, gathered)


def output_kernel(offs_ref, depth_ref, last, f_low, f_high, t_low, t_high, gathered, near, out, *scratch):
    cbuf, rows, slots = scratch
    step = pl.program_id(0)

    @pl.when(step == 0)
    def _():
        fill_slots(depth_ref, slots)
        rows[CAP:, :] = jnp.zeros((WINDOW, rows.shape[1]), bf16)
        firsts = [f_low[i] for i in range(3)] + [f_high[i] for i in range(3)]
        thirds = [t_low[0], t_high[0]]
        weight = whole_block(gathered, 2, offs_ref[depth_ref.shape[0] + 1])
        for half in range(2):
            at = slice(half * HALF, (half + 1) * HALF)
            pieces = [firsts[2 * head + half] for head in range(3)] + [thirds[half], last[half]]
            rows[at, :] = (near[at, :] + group_term(pieces, weight, cbuf)).astype(bf16)

    def body(sub, carry):
        block = step * STEP_BLOCKS + sub
        at = pl.multiple_of(sub * TOK_BLOCK, TOK_BLOCK)

        def run(start, shift_by, window):
            spread = lax.dot_general(
                window_onehot(slots, block, shift_by, window),
                rows[pl.ds(start, window), :],
                (((0,), (0,)), ((), ())),
                preferred_element_type=f32,
            )
            out[pl.ds(at, TOK_BLOCK), :] = spread.astype(bf16)

        by_window(offs_ref, block, run)
        return carry

    lax.fori_loop(0, STEP_BLOCKS, body, 0)


def output_update(offsets, depth_blocks, pieces, gathered, near, length):
    width = near.shape[1]
    blocks = length // TOK_BLOCK
    rows = STEP_BLOCKS * TOK_BLOCK

    operands = (depth_blocks, *pieces, gathered, near)
    return pl.pallas_call(
        output_kernel,
        out_shape=jax.ShapeDtypeStruct((length, width), bf16),
        grid_spec=pltpu.PrefetchScalarGridSpec(
            num_scalar_prefetch=1,
            grid=(length // rows,),
            in_specs=vmem_specs(len(operands)),
            out_specs=pl.BlockSpec((rows, width), lambda i, o: (i, 0)),
            scratch_shapes=[
                pltpu.VMEM((HALF, 5 * HD), bf16),
                pltpu.VMEM((ROOM, width), bf16),
                pltpu.VMEM((blocks, TOK_BLOCK), jnp.int32),
            ],
        ),
        compiler_params=params(16),
        cost_estimate=cost(8),
        name="output",
    )(offsets, *operands)


def shift(value, axis, distance):
    size = lax.axis_size(axis)
    return lax.ppermute(value, axis, [(i, (i + distance) % size) for i in range(size)])


def swap(value, axis, bit):
    return lax.ppermute(value, axis, [(i, i ^ bit) for i in range(lax.axis_size(axis))])


def after(value, *others):
    return lax.optimization_barrier((value, others))[0]


def ring_near(value):
    return [shift(value, "tensor", 1), shift(value, "tensor", -1)]


def ring_far(near):
    middle = near[0].shape[0] // 2
    return [shift(near[0][:middle], "tensor", 1), shift(near[1][middle:], "tensor", -1)]


def per_device(hidden, depth, qkv_weight, out_weight):
    tokens = hidden[0]
    length, width = tokens.shape
    t = lax.axis_index("tensor")
    ctx = lax.axis_index("ctx")
    depth_blocks = depth.reshape(length // TOK_BLOCK, TOK_BLOCK)
    block_counts = jnp.sum((depth_blocks >= RECURSION).astype(jnp.int32), axis=1)
    ends = jnp.arange(length // TOK_BLOCK + 1)
    offsets = jnp.sum(
        jnp.where(ends[:, None] > ends[None, :-1], block_counts[None, :], 0), axis=1
    ).astype(jnp.int32)
    count = jnp.sum(block_counts).reshape(1)
    place_both = jnp.stack([t, ctx]).astype(jnp.int32)
    weight = jnp.transpose(qkv_weight, (1, 0, 2))

    x0, x1 = compact_rows(tokens, depth_blocks, offsets)


    def column_block(rows, distance):
        start = ((t + distance) & 3) * width
        return lax.dynamic_slice_in_dim(rows, start, width, axis=rows.ndim - 1)

    own_block = column_block(out_weight, 0)
    dp = lax.axis_index("dp")
    shares = out_weight.reshape(5, SHARES, HD // SHARES, out_weight.shape[1])
    shares = lax.dynamic_slice_in_dim(shares, dp & (SHARES - 1), 1, axis=1)[:, 0]
    turned = lax.dynamic_slice_in_dim(jnp.concatenate([shares[:4], shares[:4]]), ctx, 4)
    shares = jnp.concatenate([turned, shares[4:]])

    near0 = ring_near(x0)
    count = after(count, near0)
    others = [shift(count, "ctx", s) for s in (1, 2, 3)]
    far0 = ring_far(near0)
    x1, others = after((x1, others), far0)
    place_ctx = jnp.stack([ctx.astype(jnp.int32), count[0], *[o[0] for o in others], dp.astype(jnp.int32)])
    near1 = ring_near(x1)
    first = project(place_both, x0, *near0, *far0, weight, 9)
    sent0 = [first[0]] + [shift(first[s], "ctx", s) for s in (1, 2, 3)]
    far1 = ring_far(after(near1, first))
    second = project(place_both, x1, *near1, *far1, weight, 9)
    second, shares = after((second, shares), sent0)
    moved = [shift(column_block(shares, d), "tensor", d) for d in (1, 3, 2)]
    gathered = jnp.stack(moved)[None]
    for bit in (2, 1):
        gathered = jnp.concatenate([gathered, swap(gathered, "dp", bit)])
    sent1 = [second[0]] + [shift(second[s], "ctx", s) for s in (1, 2, 3)]
    arrived = [piece for s in range(4) for piece in (sent0[s], sent1[s])]

    last = attend_last(place_ctx, (first[4], second[4]), arrived)
    lasts = [last] + ring_near(last) + [shift(last, "tensor", 2)]
    to_near, to_far = attend_main(1, after(place_ctx, last), arrived)
    back = [shift(to_near, "ctx", -1), shift(to_far, "ctx", -2)]
    to_right, own = attend_main(3, after(place_ctx, to_near, to_far, lasts), arrived)
    back.append(shift(to_right, "ctx", -3))
    own, lasts, gathered = lax.optimization_barrier((own, lasts, gathered))
    firsts = jnp.concatenate([own, back[0], back[1]])
    near = ring_near(firsts)
    third = after(back[2], near)
    firsts = [firsts] + near + ring_far(near)
    near = ring_near(third)
    thirds = [third] + near + ring_far(near)
    summed = near_terms(place_ctx, lasts[:3], firsts[:3], thirds[:3], own_block, gathered)
    pieces = [lasts[3]] + firsts[3:] + thirds[3:]
    update = output_update(
        jnp.concatenate([offsets, dp.reshape(1).astype(jnp.int32)]),
        depth_blocks,
        pieces,
        gathered,
        summed,
        length,
    )
    return update[None]


def solution(mesh):
    placed = (P("dp", "ctx", "tensor"), P("dp", "ctx"), P(None, None, "tensor"), P("tensor", None))
    return jax.shard_map(
        per_device, mesh=mesh, in_specs=placed, out_specs=P("dp", "ctx", "tensor"), check_vma=False
    )
```

time: 261 us -> 226 us (0.87)
  the two profiles are of different devices: /device:TPU:20 before, /device:TPU:18 now
where the time goes in v3:
time: 226 us; the launch traced here: 224 us
  waiting for transfers between devices  75.8 us (34%)
  Pallas kernels  61.6 us (27%)
  starting transfers between devices  51.8 us (23%)
  local copies, waits for them, and re-layouts  25.7 us (11%)
  other arithmetic  9.1 us (4%)
    ppermute x34, waiting for transfers between devices, shift(): lax.ppermute(value, axis, [(i, (i + distance) % size) for i in range(size)])  75.8 us
    ppermute x34, starting transfers between devices, shift(): lax.ppermute(value, axis, [(i, (i + distance) % size) for i in range(size)])  51.2 us
    pallas_call x2, Pallas kernels, project(): pl.pallas_call(project_kernel, out_shape=(jax.ShapeDtypeStruct((5, HALF,...  21.3 us
    unnamed x77, local copies, waits for them, and re-layouts  17.7 us
    pallas_call x2, Pallas kernels, attend_main(): pl.pallas_call(functools.partial(attend_main_kernel, first_slot), out_sha...  16.3 us
    pallas_call x1, Pallas kernels, output_update(): pl.pallas_call(output_kernel, out_shape=jax.ShapeDtypeStruct((length, wid...  7.88 us
    pallas_call x1, Pallas kernels, near_terms(): pl.pallas_call(near_terms_kernel, out_shape=jax.ShapeDtypeStruct((CAP, ow...  5.49 us
    pallas_call x1, Pallas kernels, compact_rows(): pl.pallas_call(compact_kernel, out_shape=(jax.ShapeDtypeStruct((HALF, wid...  5.46 us
  transfers between devices with their start and end apart: 36, of which 20 were waited for; matrix products, arithmetic and copies ran while one was open for 6% of the time, Pallas kernels for 22%

profile of v3, /device:TPU:18, one launch (start us, length us, event | category | flops | bytes accessed | tf_op | source)
XLA Modules:
  0.0 224.4 jit_solution(13002605737311695908)
XLA Ops:
  0.5 2.4 %fusion.1 = (s32[]{:T(128)}, s32[4096]{0:T(1024)S(1)}) fusion(s32[1,4096]{1,0:T(1,128)} %param.5, s32[]{:T(128)} %broadcast.10), kind=kLoop, calls=%fused_computation.10 | loop fusion | flops 12287 | bytes 32776 | tf_op jit(solution)/shard_map/reduce_sum | solution.py:476
  3.1 2.5 %copy-done.8 = bf16[1,4096,640]{2,1,0:T(8,128)(2,1)S(1)} copy-done((bf16[1,4096,640]{2,1,0:T(8,128)(2,1)S(1)}, bf16[1,4096,640]{2,1,0:T(8,128)(2,1)}, u32[]{:S(2)}) %copy-start.8) | copy-done | bytes 5242904
  5.6 5.5 %compact.1 = (bf16[512,640]{1,0:T(8,128)(2,1)}, bf16[512,640]{1,0:T(8,128)(2,1)S(1)}) custom-call(s32[17]{0:T(128)S(1)} %select_reduce_fusion.offs_ref, s32[16,256]{1,0:T(8,128)S(1)} %reshape.16.depth_ref, bf16[4096,640]{1,0:T(8,128)(2,1)S(1)} %bitcast.22), custom_call_target="tpu_custom_call" | custom-call | flops 8800000000 | tf_op jit(solution)/shard_map/compact/pallas_call | solution.py:104
  11.9 4.0 %collective-permute-start.1 = (bf16[512,640]{1,0:T(8,128)(2,1)}, bf16[512,640]{1,0:T(8,128)(2,1)}, u32[]{:S(2)}, u32[]{:S(2)}) collective-permute-start(bf16[512,640]{1,0:T(8,128)(2,1)} %get-tuple-element.43.x), channel_id=1, source_target_pairs={{0,3},{1,0},{2,1},{3,2},{4,7},{5,4},{6,5},{7,6},{8,11},{9,8},{10,9... | collective-permute-start | bytes 1966088 | tf_op jit(solution)/shard_map/ppermute | solution.py:445
  16.3 13.9 %collective-permute-done.1.b = bf16[512,640]{1,0:T(8,128)(2,1)} collective-permute-done((bf16[512,640]{1,0:T(8,128)(2,1)}, bf16[512,640]{1,0:T(8,128)(2,1)}, u32[]{:S(2)}, u32[]{:S(2)}) %collective-permute-start.1) | collective-permute-done | bytes 655392 | tf_op jit(solution)/shard_map/ppermute | solution.py:445
  31.3 3.8 %collective-permute-start.6 = (bf16[256,640]{1,0:T(8,128)(2,1)S(1)}, bf16[256,640]{1,0:T(8,128)(2,1)S(1)}, u32[]{:S(2)}, u32[]{:S(2)}) collective-permute-start(bf16[256,640]{1,0:T(8,128)(2,1)S(1)} %slice.54), channel_id=1, source_target_pairs={{0,3},{1,0},{2,1},{3,2},{4,7},{5,4},{6,5},{7,6},{8,11},{9,8},{10,9... | collective-permute-start | bytes 983048 | tf_op jit(solution)/shard_map/ppermute | solution.py:445
  36.7 2.9 %collective-permute-start.3 = (s32[1]{0:T(128)}, s32[1]{0:T(128)}, u32[]{:S(2)}, u32[]{:S(2)}) collective-permute-start(s32[1]{0:T(128)} %bitcast.2), channel_id=1, source_target_pairs={{0,8},{4,12},{8,0},{12,4},{1,9},{5,13},{9,1},{13,5},{2,10},{6,14},... | collective-permute-start | bytes 20 | tf_op jit(solution)/shard_map/ppermute | solution.py:445
  43.3 2.3 %collective-permute-done.5.c = bf16[256,640]{1,0:T(8,128)(2,1)S(1)} collective-permute-done((bf16[256,640]{1,0:T(8,128)(2,1)S(1)}, bf16[256,640]{1,0:T(8,128)(2,1)S(1)}, u32[]{:S(2)}, u32[]{:S(2)}) %collective-permute-start.5) | collective-permute-done | bytes 327712 | tf_op jit(solution)/shard_map/ppermute | solution.py:445
  47.6 3.8 %copy-done.6 = bf16[2560,3,640]{2,0,1:T(8,128)(2,1)S(1)} copy-done((bf16[2560,3,640]{2,0,1:T(8,128)(2,1)S(1)}, bf16[2560,3,640]{2,0,1:T(8,128)(2,1)}, u32[]{:S(2)}) %copy-start.6) | copy-done | bytes 9830424
  51.4 10.6 %project.2 = (bf16[5,512,128]{2,1,0:T(8,128)(2,1)S(1)}, bf16[5,512,128]{2,1,0:T(8,128)(2,1)S(1)}, bf16[5,512,128]{2,1,0:T(8,128)(2,1)S(1)}, bf16[5,512,128]{2,1,0:T(8,128)(2,1)S(1)}, bf16[512,128]{1,0:T(8,128)(2,1)S(1)}) custom-call(s32[2]{0:T(128)S(1)} %pad_add_fusion.1.place, bf16[512,640]{1,0:T(8,128)(2,1)} %get-tuple-element.43.x, ...), custom_call_target="tpu_custom_call" | custom-call | flops 9900000256 | tf_op jit(solution)/shard_map/project/pallas_call | solution.py:173
  62.1 2.2 collective-permute-start.10
  66.4 2.5 %collective-permute-start.13 = (bf16[5,512,128]{2,1,0:T(8,128)(2,1)S(1)}, bf16[5,512,128]{2,1,0:T(8,128)(2,1)S(1)}, u32[]{:S(2)}, u32[]{:S(2)}) collective-permute-start(bf16[5,512,128]{2,1,0:T(8,128)(2,1)S(1)} %get-tuple-element.54), channel_id=1, source_target_pairs={{0,12},{4,0},{8,4},{12,8},{1,13},{5,1},{9,5},{13,9},{2,14},{6,2},{... | collective-permute-start | bytes 1966088 | tf_op jit(solution)/shard_map/ppermute | solution.py:445
  69.2 3.4 %collective-permute-done.9.c = bf16[256,640]{1,0:T(8,128)(2,1)S(1)} collective-permute-done((bf16[256,640]{1,0:T(8,128)(2,1)S(1)}, bf16[256,640]{1,0:T(8,128)(2,1)S(1)}, u32[]{:S(2)}, u32[]{:S(2)}) %collective-permute-start.9) | collective-permute-done | bytes 327712 | tf_op jit(solution)/shard_map/ppermute | solution.py:445
  72.6 10.7 %project.3 = (bf16[5,512,128]{2,1,0:T(8,128)(2,1)S(1)}, bf16[5,512,128]{2,1,0:T(8,128)(2,1)}, bf16[5,512,128]{2,1,0:T(8,128)(2,1)}, bf16[5,512,128]{2,1,0:T(8,128)(2,1)}, bf16[512,128]{1,0:T(8,128)(2,1)S(1)}) custom-call(s32[2]{0:T(128)S(1)} %pad_add_fusion.1.place, bf16[512,640]{1,0:T(8,128)(2,1)S(1)} %copy-done.10, ...), custom_call_target="tpu_custom_call" | custom-call | flops 9900000256 | tf_op jit(solution)/shard_map/project/pallas_call | solution.py:173
  84.2 7.5 %collective-permute-done.11.refs_2_ = bf16[5,512,128]{2,1,0:T(8,128)(2,1)S(1)} collective-permute-done((bf16[5,512,128]{2,1,0:T(8,128)(2,1)S(1)}, bf16[5,512,128]{2,1,0:T(8,128)(2,1)S(1)}, u32[]{:S(2)}, u32[]{:S(2)}) %collective-permute-start.11) | collective-permute-done | bytes 655392 | tf_op jit(solution)/shard_map/ppermute | solution.py:445
  97.8 4.3 %collective-permute-start.22 = (bf16[5,32,640]{2,1,0:T(8,128)(2,1)S(1)}, bf16[5,32,640]{2,1,0:T(8,128)(2,1)S(1)}, u32[]{:S(2)}, u32[]{:S(2)}) collective-permute-start(bf16[5,32,640]{2,1,0:T(8,128)(2,1)S(1)} %get-tuple-element.84), channel_id=1, source_target_pairs={{0,2},{1,3},{2,0},{3,1},{4,6},{5,7},{6,4},{7,5},{8,10},{9,11},{10,... | collective-permute-start | bytes 614408 | tf_op jit(solution)/shard_map/ppermute | solution.py:445
  102.4 3.7 %collective-permute-done.22 = bf16[5,32,640]{2,1,0:T(8,128)(2,1)S(1)} collective-permute-done((bf16[5,32,640]{2,1,0:T(8,128)(2,1)S(1)}, bf16[5,32,640]{2,1,0:T(8,128)(2,1)S(1)}, u32[]{:S(2)}, u32[]{:S(2)}) %collective-permute-start.22) | collective-permute-done | bytes 204832 | tf_op jit(solution)/shard_map/ppermute | solution.py:445
  106.1 3.8 %collective-permute-done.21 = bf16[5,32,640]{2,1,0:T(8,128)(2,1)S(1)} collective-permute-done((bf16[5,32,640]{2,1,0:T(8,128)(2,1)S(1)}, bf16[5,32,640]{2,1,0:T(8,128)(2,1)S(1)}, u32[]{:S(2)}, u32[]{:S(2)}) %collective-permute-start.21) | collective-permute-done | bytes 204832 | tf_op jit(solution)/shard_map/ppermute | solution.py:445
  111.4 2.5 %stack.27.place = s32[6]{0:T(128)S(1)} concatenate(s32[1]{0:T(128)} %bitcast.1, s32[1]{0:T(128)} %bitcast.2, s32[1]{0:T(128)} %collective-permute-done.2, s32[1]{0:T(128)} %collective-permute-done.3, s32[1]{0:T(128)} %collective-permute-done.4, s32[1]{0:T(128)} %bitcast), dimensions={0} | concatenate | bytes 48 | tf_op jit(solution)/shard_map/stack | solution.py:499
  113.9 11.7 %collective-permute-done.15.refs_5_ = bf16[5,512,128]{2,1,0:T(8,128)(2,1)} collective-permute-done((bf16[5,512,128]{2,1,0:T(8,128)(2,1)}, bf16[5,512,128]{2,1,0:T(8,128)(2,1)}, u32[]{:S(2)}, u32[]{:S(2)}) %collective-permute-start.15) | collective-permute-done | bytes 655392 | tf_op jit(solution)/shard_map/ppermute | solution.py:445
  132.7 5.2 %attend_last.1.refs_0_ = bf16[2,512,128]{2,1,0:T(8,128)(2,1)S(1)} custom-call(s32[6]{0:T(128)S(1)} %stack.27.place, bf16[512,128]{1,0:T(8,128)(2,1)S(1)} %get-tuple-element.49.q0, bf16[512,128]{1,0:T(8,128)(2,1)S(1)} %copy-done.36, bf16[5,512,128]{2,1,0:T(8,128)(2,1)S(1)} %copy-done.30, bf16[5,512,128]{2,1,0:T(8,128)(2,1)S(1)} %copy-done.33, ...), custom_call_target="tpu_custom_call" | custom-call | flops 4400000000 | tf_op jit(solution)/shard_map/attend_last/pallas_call | solution.py:314
  137.9 3.8 %collective-permute-start.19 = (bf16[2,512,128]{2,1,0:T(8,128)(2,1)S(1)}, bf16[2,512,128]{2,1,0:T(8,128)(2,1)S(1)}, u32[]{:S(2)}, u32[]{:S(2)}) collective-permute-start(bf16[2,512,128]{2,1,0:T(8,128)(2,1)S(1)} %attend_last.1.refs_0_), channel_id=1, source_target_pairs={{0,2},{1,3},{2,0},{3,1},{4,6},{5,7},{6,4},{7,5},{8,10},{9,11},{10,... | collective-permute-start | bytes 786440 | tf_op jit(solution)/shard_map/ppermute | solution.py:445
  145.3 6.3 %attend_main.2 = (bf16[2,512,128]{2,1,0:T(8,128)(2,1)S(1)}, bf16[2,512,128]{2,1,0:T(8,128)(2,1)S(1)}) custom-call(s32[6]{0:T(128)S(1)} %stack.27.place, bf16[5,512,128]{2,1,0:T(8,128)(2,1)S(1)} %copy-done.31, bf16[5,512,128]{2,1,0:T(8,128)(2,1)S(1)} %copy-done.34, bf16[5,512,128]{2,1,0:T(8,128)(2,1)S(1)} %copy-done.13, ...), custom_call_target="tpu_custom_call" | custom-call | flops 11000000512 | tf_op jit(solution)/shard_map/attend_main/pallas_call | solution.py:272
  151.6 3.0 %collective-permute-start.25 = (bf16[2,512,128]{2,1,0:T(8,128)(2,1)S(1)}, bf16[2,512,128]{2,1,0:T(8,128)(2,1)S(1)}, u32[]{:S(2)}, u32[]{:S(2)}) collective-permute-start(bf16[2,512,128]{2,1,0:T(8,128)(2,1)S(1)} %get-tuple-element.68), channel_id=1, source_target_pairs={{0,12},{4,0},{8,4},{12,8},{1,13},{5,1},{9,5},{13,9},{2,14},{6,2},{... | collective-permute-start | bytes 786440 | tf_op jit(solution)/shard_map/ppermute | solution.py:445
  154.6 4.7 %collective-permute-start.26 = (bf16[2,512,128]{2,1,0:T(8,128)(2,1)S(1)}, bf16[2,512,128]{2,1,0:T(8,128)(2,1)S(1)}, u32[]{:S(2)}, u32[]{:S(2)}) collective-permute-start(bf16[2,512,128]{2,1,0:T(8,128)(2,1)S(1)} %get-tuple-element.69), channel_id=1, source_target_pairs={{0,8},{4,12},{8,0},{12,4},{1,9},{5,13},{9,1},{13,5},{2,10},{6,14},... | collective-permute-start | bytes 786440 | tf_op jit(solution)/shard_map/ppermute | solution.py:445
  159.3 10.0 %attend_main.3 = (bf16[2,512,128]{2,1,0:T(8,128)(2,1)S(1)}, bf16[2,512,128]{2,1,0:T(8,128)(2,1)S(1)}) custom-call(s32[6]{0:T(128)S(1)} %stack.27.place, bf16[5,512,128]{2,1,0:T(8,128)(2,1)S(1)} %copy-done.31, bf16[5,512,128]{2,1,0:T(8,128)(2,1)S(1)} %copy-done.34, bf16[5,512,128]{2,1,0:T(8,128)(2,1)S(1)} %copy-done.13, ...), custom_call_target="tpu_custom_call" | custom-call | flops 11000000512 | tf_op jit(solution)/shard_map/attend_main/pallas_call | solution.py:272
  169.4 3.0 %pad_maximum_fusion.refs_10_.gathered = bf16[4,3,5,32,640]{4,3,2,1,0:T(8,128)(2,1)} fusion(bf16[2,3,5,32,640]{4,3,2,1,0:T(8,128)(2,1)S(1)} %collective-permute-done.24, bf16[1,3,5,32,640]{4,3,2,1,0:T(8,128)(2,1)} %collective-permute-done.23, bf16[1,3,5,32,640]{4,3,2,1,0:T(8,128)(2,1)} %maximum_bitcast_fusion), kind=kLoop, calls=%fused_computation | loop fusion | flops 2457600 | bytes 4915200 | tf_op jit(solution)/shard_map/concatenate | solution.py:509
  175.5 7.9 %collective-permute-done.31.refs_6_ = bf16[2,512,128]{2,1,0:T(8,128)(2,1)} collective-permute-done((bf16[2,512,128]{2,1,0:T(8,128)(2,1)S(1)}, bf16[2,512,128]{2,1,0:T(8,128)(2,1)}, u32[]{:S(2)}, u32[]{:S(2)}) %collective-permute-start.31) | collective-permute-done | bytes 262176 | tf_op jit(solution)/shard_map/ppermute | solution.py:445
  183.4 7.7 %collective-permute-done.29.refs_5_ = bf16[6,512,128]{2,1,0:T(8,128)(2,1)} collective-permute-done((bf16[6,512,128]{2,1,0:T(8,128)(2,1)S(1)}, bf16[6,512,128]{2,1,0:T(8,128)(2,1)}, u32[]{:S(2)}, u32[]{:S(2)}) %collective-permute-start.29) | collective-permute-done | bytes 786464 | tf_op jit(solution)/shard_map/ppermute | solution.py:445
  191.1 3.1 %collective-permute-done.27.refs_4_ = bf16[6,512,128]{2,1,0:T(8,128)(2,1)} collective-permute-done((bf16[6,512,128]{2,1,0:T(8,128)(2,1)S(1)}, bf16[6,512,128]{2,1,0:T(8,128)(2,1)}, u32[]{:S(2)}, u32[]{:S(2)}) %collective-permute-start.27) | collective-permute-done | bytes 786464 | tf_op jit(solution)/shard_map/ppermute | solution.py:445
  208.9 5.5 %near_terms.1.near = f32[1024,640]{1,0:T(8,128)S(1)} custom-call(s32[6]{0:T(128)S(1)} %copy-done.5, bf16[2,512,128]{2,1,0:T(8,128)(2,1)S(1)} %copy-done.23, bf16[2,512,128]{2,1,0:T(8,128)(2,1)S(1)} %copy-done.27, bf16[2,512,128]{2,1,0:T(8,128)(2,1)S(1)} %copy-done.25, bf16[6,512,128]{2,1,0:T(8,128)(2,1)S(1)} %copy-done.3, ...), custom_call_target="tpu_custom_call" | custom-call | flops 5500000256 | tf_op jit(solution)/shard_map/near_terms/pallas_call | solution.py:370
  216.5 7.9 %output.1 = bf16[4096,640]{1,0:T(8,128)(2,1)} custom-call(s32[18]{0:T(128)S(1)} %pad_add_fusion.offs_ref, s32[16,256]{1,0:T(8,128)S(1)} %reshape.16.depth_ref, bf16[2,512,128]{2,1,0:T(8,128)(2,1)S(1)} %copy-done.21, bf16[3,512,128]{2,1,0:T(8,128)(2,1)S(1)} %collective-permute-done.28.f_low, bf16[3,512,128]{2,1,0:T(8,128)(2,1)S(1)} %collective-permute-done.30.f_high, ...), custom_call_target="tpu_custom_call" | custom-call | flops 8800000000 | tf_op jit(solution)/shard_map/output/pallas_call | solution.py:423
  (151 shorter events, 51.9 us)
Async XLA Ops:
  11.9 18.3 %collective-permute-start.1 = (bf16[512,640]{1,0:T(8,128)(2,1)}, bf16[512,640]{1,0:T(8,128)(2,1)}, u32[]{:S(2)}, u32[]{:S(2)}) collective-permute-start(bf16[512,640]{1,0:T(8,128)(2,1)} %get-tuple-element.43.x), channel_id=1, source_target_pairs={{0,3},{1,0},{2,1},{3,2},{4,7},{5,4},{6,5},{7,6},{8,11},{9,8},{10,9... | collective-permute-start | bytes 1966088 | tf_op jit(solution)/shard_map/ppermute | solution.py:445
  15.9 19.1 %collective-permute-start = (bf16[512,640]{1,0:T(8,128)(2,1)}, bf16[512,640]{1,0:T(8,128)(2,1)}, u32[]{:S(2)}, u32[]{:S(2)}) collective-permute-start(bf16[512,640]{1,0:T(8,128)(2,1)} %get-tuple-element.43.x), channel_id=1, source_target_pairs={{0,1},{1,2},{2,3},{3,0},{4,5},{5,6},{6,7},{7,4},{8,9},{9,10},{10,1... | collective-permute-start | bytes 1966088 | tf_op jit(solution)/shard_map/ppermute | solution.py:445
  31.3 12.0 %collective-permute-start.6 = (bf16[256,640]{1,0:T(8,128)(2,1)S(1)}, bf16[256,640]{1,0:T(8,128)(2,1)S(1)}, u32[]{:S(2)}, u32[]{:S(2)}) collective-permute-start(bf16[256,640]{1,0:T(8,128)(2,1)S(1)} %slice.54), channel_id=1, source_target_pairs={{0,3},{1,0},{2,1},{3,2},{4,7},{5,4},{6,5},{7,6},{8,11},{9,8},{10,9... | collective-permute-start | bytes 983048 | tf_op jit(solution)/shard_map/ppermute | solution.py:445
  36.0 9.6 %collective-permute-start.5 = (bf16[256,640]{1,0:T(8,128)(2,1)S(1)}, bf16[256,640]{1,0:T(8,128)(2,1)S(1)}, u32[]{:S(2)}, u32[]{:S(2)}) collective-permute-start(bf16[256,640]{1,0:T(8,128)(2,1)S(1)} %slice.53), channel_id=1, source_target_pairs={{0,1},{1,2},{2,3},{3,0},{4,5},{5,6},{6,7},{7,4},{8,9},{9,10},{10,1... | collective-permute-start | bytes 983048 | tf_op jit(solution)/shard_map/ppermute | solution.py:445
  45.6 16.4 %collective-permute-start.8 = (bf16[512,640]{1,0:T(8,128)(2,1)S(1)}, bf16[512,640]{1,0:T(8,128)(2,1)S(1)}, u32[]{:S(2)}, u32[]{:S(2)}) collective-permute-start(bf16[512,640]{1,0:T(8,128)(2,1)S(1)} %copy-done.10), channel_id=1, source_target_pairs={{0,3},{1,0},{2,1},{3,2},{4,7},{5,4},{6,5},{7,6},{8,11},{9,8},{10,9... | collective-permute-start | bytes 1966088 | tf_op jit(solution)/shard_map/ppermute | solution.py:445
  46.5 15.5 %collective-permute-start.7 = (bf16[512,640]{1,0:T(8,128)(2,1)S(1)}, bf16[512,640]{1,0:T(8,128)(2,1)S(1)}, u32[]{:S(2)}, u32[]{:S(2)}) collective-permute-start(bf16[512,640]{1,0:T(8,128)(2,1)S(1)} %copy-done.10), channel_id=1, source_target_pairs={{0,1},{1,2},{2,3},{3,0},{4,5},{5,6},{6,7},{7,4},{8,9},{9,10},{10,1... | collective-permute-start | bytes 1966088 | tf_op jit(solution)/shard_map/ppermute | solution.py:445
  64.3 8.3 %collective-permute-start.9 = (bf16[256,640]{1,0:T(8,128)(2,1)S(1)}, bf16[256,640]{1,0:T(8,128)(2,1)S(1)}, u32[]{:S(2)}, u32[]{:S(2)}) collective-permute-start(bf16[256,640]{1,0:T(8,128)(2,1)S(1)} %slice.43), channel_id=1, source_target_pairs={{0,1},{1,2},{2,3},{3,0},{4,5},{5,6},{6,7},{7,4},{8,9},{9,10},{10,1... | collective-permute-start | bytes 983048 | tf_op jit(solution)/shard_map/ppermute | solution.py:445
  64.4 27.3 %collective-permute-start.11 = (bf16[5,512,128]{2,1,0:T(8,128)(2,1)S(1)}, bf16[5,512,128]{2,1,0:T(8,128)(2,1)S(1)}, u32[]{:S(2)}, u32[]{:S(2)}) collective-permute-start(bf16[5,512,128]{2,1,0:T(8,128)(2,1)S(1)} %get-tuple-element.52), channel_id=1, source_target_pairs={{0,4},{4,8},{8,12},{12,0},{1,5},{5,9},{9,13},{13,1},{2,6},{6,10},{... | collective-permute-start | bytes 1966088 | tf_op jit(solution)/shard_map/ppermute | solution.py:445
  65.6 26.0 %collective-permute-start.12 = (bf16[5,512,128]{2,1,0:T(8,128)(2,1)S(1)}, bf16[5,512,128]{2,1,0:T(8,128)(2,1)S(1)}, u32[]{:S(2)}, u32[]{:S(2)}) collective-permute-start(bf16[5,512,128]{2,1,0:T(8,128)(2,1)S(1)} %get-tuple-element.53), channel_id=1, source_target_pairs={{0,8},{4,12},{8,0},{12,4},{1,9},{5,13},{9,1},{13,5},{2,10},{6,14},... | collective-permute-start | bytes 1966088 | tf_op jit(solution)/shard_map/ppermute | solution.py:445
  66.4 27.1 %collective-permute-start.13 = (bf16[5,512,128]{2,1,0:T(8,128)(2,1)S(1)}, bf16[5,512,128]{2,1,0:T(8,128)(2,1)S(1)}, u32[]{:S(2)}, u32[]{:S(2)}) collective-permute-start(bf16[5,512,128]{2,1,0:T(8,128)(2,1)S(1)} %get-tuple-element.54), channel_id=1, source_target_pairs={{0,12},{4,0},{8,4},{12,8},{1,13},{5,1},{9,5},{13,9},{2,14},{6,2},{... | collective-permute-start | bytes 1966088 | tf_op jit(solution)/shard_map/ppermute | solution.py:445
  93.6 8.6 %collective-permute-start.20 = (bf16[5,32,640]{2,1,0:T(8,128)(2,1)S(1)}, bf16[5,32,640]{2,1,0:T(8,128)(2,1)S(1)}, u32[]{:S(2)}, u32[]{:S(2)}) collective-permute-start(bf16[5,32,640]{2,1,0:T(8,128)(2,1)S(1)} %get-tuple-element.83), channel_id=1, source_target_pairs={{0,1},{1,2},{2,3},{3,0},{4,5},{5,6},{6,7},{7,4},{8,9},{9,10},{10,1... | collective-permute-start | bytes 614408 | tf_op jit(solution)/shard_map/ppermute | solution.py:445
  93.9 20.0 %collective-permute-start.14 = (bf16[5,512,128]{2,1,0:T(8,128)(2,1)}, bf16[5,512,128]{2,1,0:T(8,128)(2,1)}, u32[]{:S(2)}, u32[]{:S(2)}) collective-permute-start(bf16[5,512,128]{2,1,0:T(8,128)(2,1)} %get-tuple-element.64), channel_id=1, source_target_pairs={{0,4},{4,8},{8,12},{12,0},{1,5},{5,9},{9,13},{13,1},{2,6},{6,10},{... | collective-permute-start | bytes 1966088 | tf_op jit(solution)/shard_map/ppermute | solution.py:445
  95.7 29.9 %collective-permute-start.15 = (bf16[5,512,128]{2,1,0:T(8,128)(2,1)}, bf16[5,512,128]{2,1,0:T(8,128)(2,1)}, u32[]{:S(2)}, u32[]{:S(2)}) collective-permute-start(bf16[5,512,128]{2,1,0:T(8,128)(2,1)} %get-tuple-element.65), channel_id=1, source_target_pairs={{0,8},{4,12},{8,0},{12,4},{1,9},{5,13},{9,1},{13,5},{2,10},{6,14},... | collective-permute-start | bytes 1966088 | tf_op jit(solution)/shard_map/ppermute | solution.py:445
  96.6 29.7 %collective-permute-start.16 = (bf16[5,512,128]{2,1,0:T(8,128)(2,1)}, bf16[5,512,128]{2,1,0:T(8,128)(2,1)}, u32[]{:S(2)}, u32[]{:S(2)}) collective-permute-start(bf16[5,512,128]{2,1,0:T(8,128)(2,1)} %get-tuple-element.66), channel_id=1, source_target_pairs={{0,12},{4,0},{8,4},{12,8},{1,13},{5,1},{9,5},{13,9},{2,14},{6,2},{... | collective-permute-start | bytes 1966088 | tf_op jit(solution)/shard_map/ppermute | solution.py:445
  97.8 8.3 %collective-permute-start.22 = (bf16[5,32,640]{2,1,0:T(8,128)(2,1)S(1)}, bf16[5,32,640]{2,1,0:T(8,128)(2,1)S(1)}, u32[]{:S(2)}, u32[]{:S(2)}) collective-permute-start(bf16[5,32,640]{2,1,0:T(8,128)(2,1)S(1)} %get-tuple-element.84), channel_id=1, source_target_pairs={{0,2},{1,3},{2,0},{3,1},{4,6},{5,7},{6,4},{7,5},{8,10},{9,11},{10,... | collective-permute-start | bytes 614408 | tf_op jit(solution)/shard_map/ppermute | solution.py:445
  102.1 7.8 %collective-permute-start.21 = (bf16[5,32,640]{2,1,0:T(8,128)(2,1)S(1)}, bf16[5,32,640]{2,1,0:T(8,128)(2,1)S(1)}, u32[]{:S(2)}, u32[]{:S(2)}) collective-permute-start(bf16[5,32,640]{2,1,0:T(8,128)(2,1)S(1)} %get-tuple-element.85), channel_id=1, source_target_pairs={{0,3},{1,0},{2,1},{3,2},{4,7},{5,4},{6,5},{7,6},{8,11},{9,8},{10,9... | collective-permute-start | bytes 614408 | tf_op jit(solution)/shard_map/ppermute | solution.py:445
  110.8 32.9 %collective-permute-start.23 = (bf16[1,3,5,32,640]{4,3,2,1,0:T(8,128)(2,1)}, bf16[1,3,5,32,640]{4,3,2,1,0:T(8,128)(2,1)}, u32[]{:S(2)}, u32[]{:S(2)}) collective-permute-start(bf16[1,3,5,32,640]{4,3,2,1,0:T(8,128)(2,1)} %maximum_bitcast_fusion), channel_id=1, source_target_pairs={{0,32},{16,48},{32,0},{48,16},{64,96},{80,112},{96,64},{112,80},{1... | collective-permute-start | bytes 1843208 | tf_op jit(solution)/shard_map/ppermute | solution.py:449
  137.9 16.6 %collective-permute-start.19 = (bf16[2,512,128]{2,1,0:T(8,128)(2,1)S(1)}, bf16[2,512,128]{2,1,0:T(8,128)(2,1)S(1)}, u32[]{:S(2)}, u32[]{:S(2)}) collective-permute-start(bf16[2,512,128]{2,1,0:T(8,128)(2,1)S(1)} %attend_last.1.refs_0_), channel_id=1, source_target_pairs={{0,2},{1,3},{2,0},{3,1},{4,6},{5,7},{6,4},{7,5},{8,10},{9,11},{10,... | collective-permute-start | bytes 786440 | tf_op jit(solution)/shard_map/ppermute | solution.py:445
  141.7 17.6 %collective-permute-start.18 = (bf16[2,512,128]{2,1,0:T(8,128)(2,1)S(1)}, bf16[2,512,128]{2,1,0:T(8,128)(2,1)S(1)}, u32[]{:S(2)}, u32[]{:S(2)}) collective-permute-start(bf16[2,512,128]{2,1,0:T(8,128)(2,1)S(1)} %attend_last.1.refs_0_), channel_id=1, source_target_pairs={{0,3},{1,0},{2,1},{3,2},{4,7},{5,4},{6,5},{7,6},{8,11},{9,8},{10,9... | collective-permute-start | bytes 786440 | tf_op jit(solution)/shard_map/ppermute | solution.py:445
  141.7 17.6 %collective-permute-start.17 = (bf16[2,512,128]{2,1,0:T(8,128)(2,1)S(1)}, bf16[2,512,128]{2,1,0:T(8,128)(2,1)S(1)}, u32[]{:S(2)}, u32[]{:S(2)}) collective-permute-start(bf16[2,512,128]{2,1,0:T(8,128)(2,1)S(1)} %attend_last.1.refs_0_), channel_id=1, source_target_pairs={{0,1},{1,2},{2,3},{3,0},{4,5},{5,6},{6,7},{7,4},{8,9},{9,10},{10,1... | collective-permute-start | bytes 786440 | tf_op jit(solution)/shard_map/ppermute | solution.py:445
  145.1 24.2 %collective-permute-start.24 = (bf16[2,3,5,32,640]{4,3,2,1,0:T(8,128)(2,1)S(1)}, bf16[2,3,5,32,640]{4,3,2,1,0:T(8,128)(2,1)S(1)}, u32[]{:S(2)}, u32[]{:S(2)}) collective-permute-start(bf16[2,3,5,32,640]{4,3,2,1,0:T(8,128)(2,1)S(1)} %pad_maximum_fusion.1), channel_id=1, source_target_pairs={{0,16},{16,0},{32,48},{48,32},{64,80},{80,64},{96,112},{112,96},{1... | collective-permute-start | bytes 3686408 | tf_op jit(solution)/shard_map/ppermute | solution.py:449
  151.6 20.8 %collective-permute-start.25 = (bf16[2,512,128]{2,1,0:T(8,128)(2,1)S(1)}, bf16[2,512,128]{2,1,0:T(8,128)(2,1)S(1)}, u32[]{:S(2)}, u32[]{:S(2)}) collective-permute-start(bf16[2,512,128]{2,1,0:T(8,128)(2,1)S(1)} %get-tuple-element.68), channel_id=1, source_target_pairs={{0,12},{4,0},{8,4},{12,8},{1,13},{5,1},{9,5},{13,9},{2,14},{6,2},{... | collective-permute-start | bytes 786440 | tf_op jit(solution)/shard_map/ppermute | solution.py:445
  154.6 17.9 %collective-permute-start.26 = (bf16[2,512,128]{2,1,0:T(8,128)(2,1)S(1)}, bf16[2,512,128]{2,1,0:T(8,128)(2,1)S(1)}, u32[]{:S(2)}, u32[]{:S(2)}) collective-permute-start(bf16[2,512,128]{2,1,0:T(8,128)(2,1)S(1)} %get-tuple-element.69), channel_id=1, source_target_pairs={{0,8},{4,12},{8,0},{12,4},{1,9},{5,13},{9,1},{13,5},{2,10},{6,14},... | collective-permute-start | bytes 786440 | tf_op jit(solution)/shard_map/ppermute | solution.py:445
  172.5 18.6 %collective-permute-start.29 = (bf16[6,512,128]{2,1,0:T(8,128)(2,1)S(1)}, bf16[6,512,128]{2,1,0:T(8,128)(2,1)}, u32[]{:S(2)}, u32[]{:S(2)}) collective-permute-start(bf16[6,512,128]{2,1,0:T(8,128)(2,1)S(1)} %constant_dynamic-update-slice_fusion.refs_3_), channel_id=1, source_target_pairs={{0,3},{1,0},{2,1},{3,2},{4,7},{5,4},{6,5},{7,6},{8,11},{9,8},{10,9... | collective-permute-start | bytes 2359304 | tf_op jit(solution)/shard_map/ppermute | solution.py:445
  174.0 20.3 %collective-permute-start.27 = (bf16[6,512,128]{2,1,0:T(8,128)(2,1)S(1)}, bf16[6,512,128]{2,1,0:T(8,128)(2,1)}, u32[]{:S(2)}, u32[]{:S(2)}) collective-permute-start(bf16[6,512,128]{2,1,0:T(8,128)(2,1)S(1)} %constant_dynamic-update-slice_fusion.refs_3_), channel_id=1, source_target_pairs={{0,1},{1,2},{2,3},{3,0},{4,5},{5,6},{6,7},{7,4},{8,9},{9,10},{10,1... | collective-permute-start | bytes 2359304 | tf_op jit(solution)/shard_map/ppermute | solution.py:445
  175.5 7.9 %collective-permute-start.31 = (bf16[2,512,128]{2,1,0:T(8,128)(2,1)S(1)}, bf16[2,512,128]{2,1,0:T(8,128)(2,1)}, u32[]{:S(2)}, u32[]{:S(2)}) collective-permute-start(bf16[2,512,128]{2,1,0:T(8,128)(2,1)S(1)} %get-tuple-element.75), channel_id=1, source_target_pairs={{0,4},{4,8},{8,12},{12,0},{1,5},{5,9},{9,13},{13,1},{2,6},{6,10},{... | collective-permute-start | bytes 786440 | tf_op jit(solution)/shard_map/ppermute | solution.py:445
  194.2 9.1 %collective-permute-start.34 = (bf16[2,512,128]{2,1,0:T(8,128)(2,1)}, bf16[2,512,128]{2,1,0:T(8,128)(2,1)S(1)}, u32[]{:S(2)}, u32[]{:S(2)}) collective-permute-start(bf16[2,512,128]{2,1,0:T(8,128)(2,1)} %collective-permute-done.31.refs_6_), channel_id=1, source_target_pairs={{0,3},{1,0},{2,1},{3,2},{4,7},{5,4},{6,5},{7,6},{8,11},{9,8},{10,9... | collective-permute-start | bytes 786440 | tf_op jit(solution)/shard_map/ppermute | solution.py:445
  194.2 10.4 %collective-permute-start.32 = (bf16[2,512,128]{2,1,0:T(8,128)(2,1)}, bf16[2,512,128]{2,1,0:T(8,128)(2,1)}, u32[]{:S(2)}, u32[]{:S(2)}) collective-permute-start(bf16[2,512,128]{2,1,0:T(8,128)(2,1)} %collective-permute-done.31.refs_6_), channel_id=1, source_target_pairs={{0,1},{1,2},{2,3},{3,0},{4,5},{5,6},{6,7},{7,4},{8,9},{9,10},{10,1... | collective-permute-start | bytes 786440 | tf_op jit(solution)/shard_map/ppermute | solution.py:445
  198.3 16.0 %collective-permute-start.30 = (bf16[3,512,128]{2,1,0:T(8,128)(2,1)S(1)}, bf16[3,512,128]{2,1,0:T(8,128)(2,1)S(1)}, u32[]{:S(2)}, u32[]{:S(2)}) collective-permute-start(bf16[3,512,128]{2,1,0:T(8,128)(2,1)S(1)} %slice.56), channel_id=1, source_target_pairs={{0,3},{1,0},{2,1},{3,2},{4,7},{5,4},{6,5},{7,6},{8,11},{9,8},{10,9... | collective-permute-start | bytes 1179656 | tf_op jit(solution)/shard_map/ppermute | solution.py:445
  200.6 15.8 %collective-permute-start.28 = (bf16[3,512,128]{2,1,0:T(8,128)(2,1)S(1)}, bf16[3,512,128]{2,1,0:T(8,128)(2,1)S(1)}, u32[]{:S(2)}, u32[]{:S(2)}) collective-permute-start(bf16[3,512,128]{2,1,0:T(8,128)(2,1)S(1)} %slice.55), channel_id=1, source_target_pairs={{0,1},{1,2},{2,3},{3,0},{4,5},{5,6},{6,7},{7,4},{8,9},{9,10},{10,1... | collective-permute-start | bytes 1179656 | tf_op jit(solution)/shard_map/ppermute | solution.py:445
  203.3 11.2 %collective-permute-start.35 = (bf16[1,512,128]{2,1,0:T(8,128)(2,1)S(1)}, bf16[1,512,128]{2,1,0:T(8,128)(2,1)S(1)}, u32[]{:S(2)}, u32[]{:S(2)}) collective-permute-start(bf16[1,512,128]{2,1,0:T(8,128)(2,1)S(1)} %slice.58), channel_id=1, source_target_pairs={{0,3},{1,0},{2,1},{3,2},{4,7},{5,4},{6,5},{7,6},{8,11},{9,8},{10,9... | collective-permute-start | bytes 393224 | tf_op jit(solution)/shard_map/ppermute | solution.py:445
  205.5 11.0 %collective-permute-start.33 = (bf16[1,512,128]{2,1,0:T(8,128)(2,1)S(1)}, bf16[1,512,128]{2,1,0:T(8,128)(2,1)S(1)}, u32[]{:S(2)}, u32[]{:S(2)}) collective-permute-start(bf16[1,512,128]{2,1,0:T(8,128)(2,1)S(1)} %slice.57), channel_id=1, source_target_pairs={{0,1},{1,2},{2,3},{3,0},{4,5},{5,6},{6,7},{7,4},{8,9},{9,10},{10,1... | collective-permute-start | bytes 393224 | tf_op jit(solution)/shard_map/ppermute | solution.py:445
  (41 other events, 412.6 us)
